TPU v7x, 128 devices: a whole 4x4x4 slice. The times are simulated.
128 devices in a mesh: azimuth: 16 (over y_hi, z, core), radius: 8 (over x, y_lo).
Axes of the slice: x: 4, y: 4 (y_hi: 2, y_lo: 2; y = y_hi * 2 + y_lo), z: 4, core: 2. Of those that a mesh axis runs over, the one named last changes fastest.
Arguments:
- flow_state: float32 [5, 256, 256, 384], P(None, 'azimuth', 'radius'), may hold values from -6 to 6
- base_state: float32 [5, 256, 256, 384], P(None, 'azimuth', 'radius'), may hold values from -6 to 6
- mean_flow: float32 [2, 256], P(None, 'radius'), may hold values from 0.1 to 0.5
- panel_history: bfloat16 [16, 8, 16, 2016], P('azimuth', 'radius'), may hold values from -6 to 6
- panel_line: int32 [16, 8, 16], P('azimuth', 'radius'), may hold values from 0 to 511
- panel_start: int32 [16, 8, 16], P('azimuth', 'radius'), may hold values from 0 to 352
- panel_count: int32 [16, 8], replicated, may hold values from 2 to 16, as said below
- panel_owner: int32 [16, 8, 16], replicated, may hold values from 0 to 15, as said below
- source_weight: bfloat16 [8, 16384, 4096], P('radius', 'azimuth'), may hold values from -0.046875 to 0.046875
- retarded_time: float32 [128, 64, 64], replicated, may hold values from -0.75 to 0.75
- observer_block: int32 [128], replicated, may hold values from 0 to 127, each once
Outputs:
- next_state: float32 [5, 256, 256, 384], P(None, 'azimuth', 'radius')
- observer_pressure: float32 [128, 2048], P(('azimuth', 'radius'))
Inputs may be any that keep to these rules, and one draw needn't show every extreme that they name: The slots 0 to panel_count[a, b] - 1 of device (a, b) are live. `panel_owner`: entries of slots that are not live are ignored. At most 2 live blocks of one device go to one owner, and in every radius band some owner receives exactly 2 live blocks from every device of the band.
All inputs are finite; a program needn't handle non-finite values.
Results may differ from a plain program's by a relative error of at most 0.00039.
Values may be sent and summed in bfloat16 or wider, within the bound.
No kernel may reach another device: no remote copies, remote signals or barrier semaphores. Data moves between devices by JAX's collectives and lax.ppermute only.
A program may use at most 192 MiB of HBM per device.

v0:
```python
import math

import jax
import jax.numpy as jnp
from jax import lax
from jax.sharding import PartitionSpec as P

NT = 64
BP = 32
KMAX = 16
CAP = 2
OBS = 4096


SECTION_STEP = 0.3
VISCOSITY = 0.05


def extended_2(value, sides, width, wrap):
    for axis, dim in sides:
        count, length = (lax.axis_size(axis), value.shape[dim])
        up = [(i, (i + 1) % count) for i in range(count if wrap else count - 1)]
        down = [(j, i) for i, j in up]
        last = lax.slice_in_dim(value, length - width, length, axis=dim)
        leading = lax.slice_in_dim(value, 0, width, axis=dim)
        before = lax.ppermute(last, axis, up)
        after = lax.ppermute(leading, axis, down)
        value = jnp.concatenate([before, value, after], axis=dim)
    return value


def first_diff(extended, axis_dim, length):

    def shifted(offset):
        return lax.slice_in_dim(extended, 2 + offset, 2 + offset + length, axis=axis_dim)

    return (8.0 * (shifted(1) - shifted(-1)) - (shifted(2) - shifted(-2))) / 12.0


def second_diff(extended, axis_dim, length):

    def shifted(offset):
        return lax.slice_in_dim(extended, 2 + offset, 2 + offset + length, axis=axis_dim)

    return (
        16.0 * (shifted(1) + shifted(-1)) - (shifted(2) + shifted(-2)) - 30.0 * shifted(0)
    ) / 12.0


def tendency(fields, cycle_ext, band_ext, mean_flow, radius_pos, arc_factor):
    cycle_length = fields.shape[1]
    band_length = fields.shape[2]
    axial_length = fields.shape[3]
    axial_ext = jnp.pad(fields, ((0, 0), (0, 0), (0, 0), (2, 2)))
    cycle_diff = first_diff(cycle_ext, 1, cycle_length)
    band_diff = first_diff(band_ext, 2, band_length)
    axial_diff = first_diff(axial_ext, 3, axial_length)
    smoothing = (
        second_diff(cycle_ext, 1, cycle_length)
        + second_diff(band_ext, 2, band_length)
        + second_diff(axial_ext, 3, axial_length)
    )
    swirl_flow = mean_flow[0][:, None]
    axial_flow = mean_flow[1][:, None]
    metric = arc_factor[:, None]
    inverse = 1.0 / radius_pos[:, None]
    carried = swirl_flow * metric * cycle_diff + axial_flow * axial_diff
    spread = metric * cycle_diff[1] + band_diff[2] + fields[2] * inverse + axial_diff[3]
    forcing = jnp.stack([spread, metric * cycle_diff[4], band_diff[4], axial_diff[4], spread])
    return VISCOSITY * smoothing - carried - forcing


def per_device(
    flow_state,
    base_state,
    mean_flow,
    panel_history,
    panel_line,
    panel_start,
    panel_count,
    panel_owner,
    source_weight,
    retarded_time,
    observer_block,
):
    cycle_size = lax.axis_size("azimuth")
    band_size = lax.axis_size("radius")
    cycle_cells = flow_state.shape[1]
    band_cells = flow_state.shape[2]
    axial_cells = flow_state.shape[3]
    cycle_index = lax.axis_index("azimuth")
    band_index = lax.axis_index("radius")
    cycle_total = cycle_cells * cycle_size
    band_total = band_cells * band_size
    radial_cell = band_index * band_cells + jnp.arange(band_cells, dtype=jnp.int32)
    radius_pos = radial_cell.astype(jnp.float32) + (0.5 * band_total + 0.5)
    arc_factor = cycle_total / (2.0 * math.pi) / radius_pos
    cycle_ext = extended_2(flow_state, (("azimuth", 1),), 2, True)
    band_ext = extended_2(flow_state, (("radius", 2),), 2, False)
    next_state = base_state + SECTION_STEP * tendency(
        flow_state, cycle_ext, band_ext, mean_flow, radius_pos, arc_factor
    )
    pressure_lines = next_state[4].reshape(cycle_cells * band_cells, axial_cells)

    def cut_window(line_index, start_index):
        return lax.dynamic_slice(pressure_lines, (line_index, start_index), (1, BP))[0]

    fresh_panels = jax.vmap(cut_window)(panel_line[0, 0], panel_start[0, 0])
    blocks = jnp.concatenate([panel_history[0, 0], fresh_panels.astype(jnp.bfloat16)], axis=1)
    band_owner = lax.dynamic_index_in_dim(panel_owner, band_index, 1, keepdims=False)
    band_count = lax.dynamic_index_in_dim(panel_count, band_index, 1, keepdims=False)
    slot_ids = jnp.arange(KMAX, dtype=jnp.int32)
    alive_slots = slot_ids[None, :] < band_count[:, None]
    earlier = slot_ids[:, None] < slot_ids[None, :]
    matches = (
        (band_owner[:, :, None] == band_owner[:, None, :]) & alive_slots[:, :, None] & earlier[None]
    )
    ranking = jnp.sum(matches.astype(jnp.int32), axis=1)
    slot_places = jnp.arange(CAP, dtype=jnp.int32)
    own_owner = lax.dynamic_index_in_dim(band_owner, cycle_index, 0, keepdims=False)
    own_alive = lax.dynamic_index_in_dim(alive_slots, cycle_index, 0, keepdims=False)
    own_rank = lax.dynamic_index_in_dim(ranking, cycle_index, 0, keepdims=False)
    owner_ids = jnp.arange(cycle_size, dtype=jnp.int32)
    selection = (
        own_alive[None, None, :]
        & (own_owner[None, None, :] == owner_ids[:, None, None])
        & (own_rank[None, None, :] == slot_places[None, :, None])
    )
    outgoing = jnp.einsum(
        "qck,kf->qcf", selection.astype(jnp.bfloat16), blocks, preferred_element_type=jnp.float32
    ).astype(jnp.bfloat16)
    stations = lax.all_to_all(outgoing, "azimuth", split_axis=0, concat_axis=0, tiled=True)
    total_stations = cycle_size * CAP
    weights = source_weight[0].reshape(total_stations, BP, OBS)
    partial_value = jnp.einsum(
        "stp,spo->to",
        stations.reshape(total_stations, NT, BP),
        weights,
        preferred_element_type=jnp.float32,
    )
    block_count = retarded_time.shape[0]
    block_width = OBS // block_count
    grouped = partial_value.reshape(NT, block_count, block_width)
    ordered = jnp.take(grouped, observer_block, axis=1)
    owned_sum = lax.psum_scatter(
        ordered, ("azimuth", "radius"), scatter_dimension=1, tiled=True
    ).reshape(NT, block_width)
    device_index = lax.axis_index(("azimuth", "radius"))
    chosen = lax.dynamic_index_in_dim(observer_block, device_index, 0, keepdims=False)
    matrix = lax.dynamic_index_in_dim(retarded_time, chosen, 0, keepdims=False)
    pressure = jnp.dot(
        matrix, owned_sum, precision=lax.Precision.HIGHEST, preferred_element_type=jnp.float32
    )
    return (next_state, pressure.reshape(1, NT * block_width))


def solution(mesh):
    placed = (
        P(None, "azimuth", "radius", None),
        P(None, "azimuth", "radius", None),
        P(None, "radius"),
        P("azimuth", "radius", None, None),
        P("azimuth", "radius", None),
        P("azimuth", "radius", None),
        P(),
        P(),
        P("radius", "azimuth", None),
        P(),
        P(),
    )
    return jax.shard_map(
        per_device,
        mesh=mesh,
        in_specs=placed,
        out_specs=(P(None, "azimuth", "radius", None), P(("azimuth", "radius"), None)),
        check_vma=False,
    )
```

profile of v0, /device:TPU:0, one launch (start us, length us, event | category | flops | bytes accessed | tf_op | source)
XLA Modules:
  0.0 881.2 jit_solution(18309906498322855814)
XLA Ops:
  9.1 4.5 collective-permute-start.3
  15.5 2.2 fusion.24
  17.8 5.6 collective-permute-start
  23.4 2.3 constant_dynamic-update-slice_fusion.5
  31.3 4.1 collective-permute-done.1
  35.4 18.5 %constant_dynamic-update-slice_fusion.2 = (f32[5,18,32,384]{3,2,1,0:T(8,128)S(1)}, f32[5,16,32,384]{3,2,1,0:T(8,128)}, f32[5,18,32,384]{3,2,1,0:T(8,128)S(1)}, f32[5,16,32,384]{3,2,1,0:T(8,128)}, f32[5,16,32,384]{3,2,1,0:T(8,128)}) fusion(f32[5,16,32,384]{3,2,1,0:T(8,128)} %param.11, f32[5,16,2,384]{3,2,1,0:T(2,128)S(1)} %copy.37, ...), kind=kLoop, calls=%fused_computation.41 | loop fusion | flops 11796479 | bytes 31703040
  54.0 2.0 copy-done.1
  56.0 7.8 broadcast_multiply_fusion.1
  63.8 3.1 constant_dynamic-update-slice_fusion.7
  67.0 2.3 fusion.4
  69.3 2.1 slice_dynamic-update-slice_fusion.1
  71.4 2.1 slice_dynamic-update-slice_fusion
  74.4 20.9 %fusion.3 = f32[5,16,32,384]{3,2,1,0:T(8,128)} fusion(f32[5,16,32,384]{3,2,1,0:T(8,128)} %param.12, f32[5,16,32,384]{3,2,1,0:T(8,128)} %constant_dynamic-update-slice_fusion.6, f32[5,16,32,384]{3,2,1,0:T(8,128)} %get-tuple-element.32, f32[5,16,32,384]{3,2,1,0:T(8,128)} %get-tuple-element.21, f32[5,16,32,384]{3,2,1,0:T(8,128)} %param.11, ...), kind=kLoop, calls=%fused_computation.15 | loop fusion | flops 27525120 | bytes 47431936 | tf_op jit(solution)/shard_map/add | solution.py:100
  96.5 31.4 %while.1 = (s32[]{:T(128)}, f32[512,384]{1,0:T(8,128)S(1)}, s32[16,2]{0,1:T(2,128)S(1)}, f32[16,1,32]{2,1,0:T(1,128)S(1)}, s32[]{:T(128)}) while((s32[]{:T(128)}, f32[512,384]{1,0:T(8,128)S(1)}, s32[16,2]{0,1:T(2,128)S(1)}, f32[16,1,32]{2,1,0:T(1,128)S(1)}, s32[]{:T(128)}) %tuple.39), condition=%wide.while_cond, body=%wide.while_body.sunk | while | flops 2 | bytes 1141 | solution.py:106
  128.9 3.5 all-to-all-start
  132.6 11.2 %copy.55 = bf16[32,32,4096]{2,0,1:T(8,128)(2,1)} copy(bf16[32,32,4096]{2,1,0:T(8,128)(2,1)} %bitcast.60) | data formatting | bytes 16777216 | tf_op jit(solution)/shard_map/reshape;squeeze | solution.py:134
  143.8 32.9 %dot_general.15 = bf16[128,32,32,32]{1,0,3,2:T(8,128)(2,1)} reshape(bf16[4096,32,32]{0,2,1:T(8,128)(2,1)} %bitcast.59) | data formatting | bytes 16777216 | tf_op jit(solution)/shard_map/stp,spo->to/dot_general | solution.py:135
  176.7 31.0 %copy.43 = bf16[128,32,32,32]{0,2,3,1:T(8,128)(2,1)} copy(bf16[128,32,32,32]{1,0,3,2:T(8,128)(2,1)} %dot_general.15) | data formatting | bytes 16777216 | tf_op jit(solution)/shard_map/stp,spo->to/dot_general | solution.py:135
  208.8 5.4 convolution_bitcast_fusion
  214.2 2.8 copy.44
  217.0 3.6 gather_fusion
  220.6 3.1 select_bitcast_fusion
  228.2 2.3 copy.52
  230.5 642.3 %reduce-scatter.2.cloned.1.call-done = f32[64,1,32]{0,2,1:T(8,128)} async-done(((f32[64,128,32]{0,2,1:T(8,128)}), f32[64,1,32]{0,2,1:T(8,128)}) %reduce-scatter.2.cloned.1.call-update) | async-done | bytes 8208 | tf_op jit(solution)/shard_map/reduce_scatter | solution.py:145
  (109 shorter events, 49.3 us)
Async XLA Ops:
  7.2 219.1 %copy-start = (f32[128,64,64]{0,2,1:T(8,128)S(1)}, f32[128,64,64]{0,2,1:T(8,128)}, u32[]{:S(2)}) copy-start(f32[128,64,64]{0,2,1:T(8,128)} %param.20) | copy-start | bytes 6291460
  7.2 16.2 %copy-start.3 = (f32[5,16,32,384]{3,2,1,0:T(8,128)S(1)}, f32[5,16,32,384]{3,2,1,0:T(8,128)}, u32[]{:S(2)}) copy-start(f32[5,16,32,384]{3,2,1,0:T(8,128)} %param.11) | copy-start | bytes 11796484
  9.1 19.3 %collective-permute-start.3 = (f32[5,16,2,384]{3,1,2,0:T(8,128)S(1)}, f32[5,16,2,384]{3,1,2,0:T(8,128)}, u32[]{:S(2)}, u32[]{:S(2)}) collective-permute-start(f32[5,16,2,384]{3,1,2,0:T(8,128)S(1)} %copy.51), channel_id=1, source_target_pairs={{0,1},{1,2},{2,3},{3,4},{4,5},{5,6},{6,7},{8,9},{9,10},{10,11},{11... | collective-permute-start | bytes 737288 | tf_op jit(solution)/shard_map/ppermute | solution.py:26
  14.2 15.2 %collective-permute-start.2 = (f32[5,16,2,384]{3,1,2,0:T(8,128)}, f32[5,16,2,384]{3,1,2,0:T(8,128)}, u32[]{:S(2)}, u32[]{:S(2)}) collective-permute-start(f32[5,16,2,384]{3,1,2,0:T(8,128)} %copy.50), channel_id=1, source_target_pairs={{1,0},{2,1},{3,2},{4,3},{5,4},{6,5},{7,6},{9,8},{10,9},{11,10},{12... | collective-permute-start | bytes 737288 | tf_op jit(solution)/shard_map/ppermute | solution.py:27
  17.7 17.6 %collective-permute-start.1 = (f32[5,2,32,384]{3,2,1,0:T(8,128)}, f32[5,2,32,384]{3,2,1,0:T(8,128)S(1)}, u32[]{:S(2)}, u32[]{:S(2)}) collective-permute-start(f32[5,2,32,384]{3,2,1,0:T(8,128)} %get-tuple-element.27), channel_id=1, source_target_pairs={{0,8},{8,16},{16,24},{24,32},{32,40},{40,48},{48,56},{56,64},{64,7... | collective-permute-start | bytes 1474568 | tf_op jit(solution)/shard_map/ppermute | solution.py:26
  17.7 8.0 copy-start.7
  17.7 9.9 %copy-start.8 = (s32[128]{0:T(128)S(1)}, s32[128]{0:T(128)}, u32[]{:S(2)}) copy-start(s32[128]{0:T(128)} %param.21) | copy-start | bytes 1540
  17.7 9.9 %copy-start.5 = (s32[1,1,16]{2,1,0:T(1,128)S(1)}, s32[1,1,16]{2,1,0:T(1,128)}, u32[]{:S(2)}) copy-start(s32[1,1,16]{2,1,0:T(1,128)} %param.16) | copy-start | bytes 196
  17.7 9.9 %copy-start.6 = (s32[1,1,16]{2,1,0:T(1,128)S(1)}, s32[1,1,16]{2,1,0:T(1,128)}, u32[]{:S(2)}) copy-start(s32[1,1,16]{2,1,0:T(1,128)} %param.15) | copy-start | bytes 196
  17.8 36.1 %collective-permute-start = (f32[5,2,32,384]{3,2,1,0:T(8,128)}, f32[5,2,32,384]{3,2,1,0:T(8,128)S(1)}, u32[]{:S(2)}, u32[]{:S(2)}) collective-permute-start(f32[5,2,32,384]{3,2,1,0:T(8,128)} %get-tuple-element.26), channel_id=1, source_target_pairs={{8,0},{16,8},{24,16},{32,24},{40,32},{48,40},{56,48},{64,56},{72,6... | collective-permute-start | bytes 1474568 | tf_op jit(solution)/shard_map/ppermute | solution.py:27
  53.9 2.1 copy-start.1
  67.0 7.5 copy-start.2
  74.4 53.5 %copy-start.4 = (bf16[1,1,16,2016]{3,2,1,0:T(8,128)(2,1)S(1)}, bf16[1,1,16,2016]{3,2,1,0:T(8,128)(2,1)}, u32[]{:S(2)}) copy-start(bf16[1,1,16,2016]{3,2,1,0:T(8,128)(2,1)} %param.14) | copy-start | bytes 193540
  128.9 78.8 %all-to-all-start = ((bf16[16,2,2048]{2,1,0:T(2,128)(2,1)}), bf16[16,2,2048]{2,1,0:T(2,128)(2,1)S(1)}, u32[]{:S(2)}, u32[]{:S(2)}) async-start(bf16[16,2,2048]{2,1,0:T(2,128)(2,1)} %copy.40), calls=%async_computation | async-start | bytes 262144 | tf_op jit(solution)/shard_map/all_to_all | solution.py:132
  132.4 740.4 %reduce-scatter.2.cloned.1.call-start = ((), (), s32[]{:S(2)}) async-start(), calls=%async_computation.2 | async-start | bytes 2113536 | tf_op jit(solution)/shard_map/reduce_scatter | solution.py:145
Sparse Core Ops, SparseCore 0:
  223.9 648.8 reduce-scatter.1
where the time goes:
time: 884 us; the launch traced here: 881 us
  waiting for transfers between devices  646 us (73%)
  local copies, waits for them, and re-layouts  141 us (16%)
  other arithmetic  56.1 us (6%)
  between operations  16.3 us (2%)
  starting transfers between devices  15.1 us (2%)
    reduce_scatter x1, waiting for transfers between devices, per_device(): lax.psum_scatter(ordered, ('azimuth', 'radius'), scatter_dimension=1, til...  642 us
    dot_general x3, local copies, waits for them, and re-layouts, per_device(): jnp.einsum('stp,spo->to', stations.reshape(total_stations, NT, BP), weigh...  66.7 us
    gather x48, local copies, waits for them, and re-layouts  31.3 us
    unnamed x4, other arithmetic  24 us
    add x1, other arithmetic, per_device(): base_state + SECTION_STEP * tendency(flow_state, cycle_ext, band_ext, mea...  20.9 us
  transfers between devices with their start and end apart: 6, of which 2 were waited for; matrix products, arithmetic and copies ran while one was open for 12% of the time, Pallas kernels for 0%

commit v1 on v0

v1 whole, which is shorter than its diff:
```python
import functools
import math

import jax
import jax.numpy as jnp
from jax import lax
from jax.experimental import pallas as pl
from jax.experimental.pallas import tpu as pltpu
from jax.sharding import PartitionSpec as P

NT = 64
BP = 32
KMAX = 16
CAP = 2
LANES = 128
ROWS = NT * BP // LANES
QUADS = LANES // BP

SECTION_STEP = 0.3
VISCOSITY = 0.05
BOTH = ("azimuth", "radius")

FIRST_AZ = (1, 4)
FIRST_RAD = (2, 4)
LATER_AZ = (0, 2, 3)
LATER_RAD = (0, 1, 3)


def swap_quads(tiles):
    lane = lax.broadcasted_iota(jnp.int32, tiles[0].shape, 1)
    low, even = (lane % 128) < 64, (lane % 64) < 32
    a0, a1, a2, a3 = tiles

    def turn(x, shift):
        return pltpu.roll(x, shift, 1)

    b0 = jnp.where(low, a0, turn(a2, 64))
    b2 = jnp.where(low, turn(a0, 64), a2)
    b1 = jnp.where(low, a1, turn(a3, 64))
    b3 = jnp.where(low, turn(a1, 64), a3)
    return (
        jnp.where(even, b0, turn(b1, 32)),
        jnp.where(even, turn(b0, 96), b1),
        jnp.where(even, b2, turn(b3, 32)),
        jnp.where(even, turn(b2, 96), b3),
    )


def wide(tile, length):
    return jnp.concatenate([tile] * (length // tile.shape[1]), axis=1)


def tall(tile, length):
    return jnp.concatenate([tile] * (length // tile.shape[0]), axis=0)


def radial_shifts(x, lo, hi):
    n = x.shape[0]
    row = lax.broadcasted_iota(jnp.int32, (8, x.shape[1]), 0)
    m1, m2 = pltpu.roll(x, 1, 0), pltpu.roll(x, 2, 0)
    p1, p2 = pltpu.roll(x, n - 1, 0), pltpu.roll(x, n - 2, 0)
    m1 = jnp.concatenate([jnp.where(row == 0, lo[1], m1[:8]), m1[8:]], axis=0)
    m2 = jnp.concatenate(
        [jnp.where(row == 0, lo[0], jnp.where(row == 1, lo[1], m2[:8])), m2[8:]], axis=0
    )
    p1 = jnp.concatenate([p1[:-8], jnp.where(row == 7, hi[0], p1[-8:])], axis=0)
    p2 = jnp.concatenate(
        [p2[:-8], jnp.where(row == 6, hi[0], jnp.where(row == 7, hi[1], p2[-8:]))], axis=0
    )
    return p1, m1, p2, m2


def axial_shifts(x):
    n = x.shape[1]
    return (
        pltpu.roll(x, n - 1, 1),
        pltpu.roll(x, 1, 1),
        pltpu.roll(x, n - 2, 1),
        pltpu.roll(x, 2, 1),
    )


def new_plane(var, base, plane, layers, coef, axial_coef, edge_coef):
    rows, length = base.shape
    k8, k1 = SECTION_STEP * 8.0 / 12.0, SECTION_STEP / 12.0

    def row_coef(i):
        return wide(coef[i], length)

    def edge(i):
        return tall(edge_coef[i], rows)

    x = plane(var, 0)
    rp1, rm1, rp2, rm2 = radial_shifts(x, *layers(var))
    zp1, zm1, zp2, zm2 = axial_shifts(x)
    total = base + (-3.0 * 30.0 / 12.0 * SECTION_STEP * VISCOSITY) * x
    total += row_coef(0) * plane(var, 1) + row_coef(1) * plane(var, -1)
    total += row_coef(2) * plane(var, 2) + row_coef(3) * plane(var, -2)
    total += axial_coef[0] * zp1 + axial_coef[1] * zm1
    total += axial_coef[2] * zp2 + axial_coef[3] * zm2
    total += (SECTION_STEP * VISCOSITY * 16.0 / 12.0) * (rp1 + rm1)
    total -= (SECTION_STEP * VISCOSITY / 12.0) * (rp2 + rm2)
    if var in (0, 4):
        total -= row_coef(4) * (plane(1, 1) - plane(1, -1)) - row_coef(5) * (
            plane(1, 2) - plane(1, -2)
        )
        u = plane(2, 0)
        sp1, sm1, sp2, sm2 = radial_shifts(u, *layers(2))
        total -= k8 * (sp1 - sm1) - k1 * (sp2 - sm2) + row_coef(6) * u
        wp1, wm1, wp2, wm2 = axial_shifts(plane(3, 0))
        total -= edge(0) * wp1 - edge(1) * wm1 - edge(2) * wp2 + edge(3) * wm2
    elif var == 1:
        total -= row_coef(4) * (plane(4, 1) - plane(4, -1)) - row_coef(5) * (
            plane(4, 2) - plane(4, -2)
        )
    elif var == 2:
        sp1, sm1, sp2, sm2 = radial_shifts(plane(4, 0), *layers(4))
        total -= k8 * (sp1 - sm1) - k1 * (sp2 - sm2)
    else:
        wp1, wm1, wp2, wm2 = axial_shifts(plane(4, 0))
        total -= edge(0) * wp1 - edge(1) * wm1 - edge(2) * wp2 + edge(3) * wm2
    return total


def plane_copies(flow_ref, before_ref, after_ref, ext_ref, sems, variables, planes):
    def copies(spot):
        out = []
        for slot, (var, halo_slot, halo) in enumerate(variables):
            if isinstance(spot, int) and spot < 2:
                src = before_ref[halo].at[halo_slot, spot]
            elif isinstance(spot, int) and spot >= planes + 2:
                src = after_ref[halo].at[halo_slot, spot - planes - 2]
            else:
                src = flow_ref.at[var, spot - 2]
            out.append(pltpu.make_async_copy(src, ext_ref.at[slot, spot], sems.at[slot, spot]))
        return out

    return copies


def feed_planes(a, planes, copies):
    @pl.when(a == 0)
    def _():
        for spot in (0, 1):
            for c in copies(spot):
                c.start()
        for spot in range(2, planes + 2):
            for c in copies(spot):
                c.start()
        for spot in (planes + 2, planes + 3):
            for c in copies(spot):
                c.start()
        for spot in range(4):
            for c in copies(spot):
                c.wait()

    @pl.when(a + 4 < planes + 2)
    def _():
        for c in copies(a + 4):
            c.wait()

    for spot in (planes + 2, planes + 3):

        @pl.when(a + 4 == spot)
        def _():
            for c in copies(spot):
                c.wait()


def pressure_kernel(
    meta_ref,
    flow_ref,
    before_ref,
    after_ref,
    ur_ref,
    uz_ref,
    base_ref,
    lo_ref,
    hi_ref,
    coef_ref,
    axial_ref,
    edge_ref,
    history_ref,
    next_ref,
    out_ref,
    ext_ref,
    field_ref,
    wide_ref,
    block_ref,
    rank_ref,
    sems,
):
    a = pl.program_id(0)
    planes = pl.num_programs(0)
    n = field_ref.shape[0]
    variables = [(var, slot, 0) for slot, var in enumerate(FIRST_AZ)]
    copies = plane_copies(flow_ref, (before_ref,), (after_ref,), ext_ref, sems, variables, n)
    feed_planes(a, n, copies)

    def plane(var, offset):
        if var in FIRST_AZ:
            return ext_ref[FIRST_AZ.index(var), a + 2 + offset]
        return (ur_ref if var == 2 else uz_ref)[0, 0]

    def layers(var):
        s = FIRST_RAD.index(var)
        return (
            [lo_ref[s, a, j : j + 1, :] for j in (0, 1)],
            [hi_ref[s, a, j : j + 1, :] for j in (0, 1)],
        )

    value = new_plane(4, base_ref[0, 0], plane, layers, coef_ref, axial_ref, edge_ref)
    next_ref[0, 0] = value
    tiles = field_ref.shape[1]
    for t in range(tiles):
        field_ref[a, t] = value[:, t * LANES : (t + 1) * LANES]

    @pl.when(a == planes - 1)
    def _():
        band = field_ref.shape[2]
        for r in range(ROWS):
            width = min(LANES, history_ref.shape[1] - r * LANES)
            chunk = history_ref[:, r * LANES : r * LANES + width]
            wide_ref[r, :, 0:width] = chunk.astype(jnp.float32)
        out_ref[...] = jnp.zeros_like(out_ref)
        owners = out_ref.shape[0]
        for q in range(owners):
            rank_ref[q] = 0
        lane = lax.broadcasted_iota(jnp.int32, (1, LANES), 1)

        def one(k, carry):
            @pl.when(k < meta_ref[3 * KMAX])
            def _():
                owner = meta_ref[k]
                line = meta_ref[KMAX + k]
                start = meta_ref[2 * KMAX + k]
                rank = rank_ref[owner]
                rank_ref[owner] = rank + 1
                for r in range(ROWS):
                    block_ref[r : r + 1, :] = wide_ref[r, pl.ds(k, 1), :]
                tile = start // LANES
                off = start % LANES
                other = jnp.minimum(tile + 1, tiles - 1)
                at = pl.ds(line % band, 1)
                x0 = field_ref[line // band, tile, at, :]
                x1 = field_ref[line // band, other, at, :]
                shift = (2 * LANES - BP - off) % LANES
                r0 = pltpu.roll(jnp.broadcast_to(x0, (8, LANES)), shift, 1)[0:1]
                r1 = pltpu.roll(jnp.broadcast_to(x1, (8, LANES)), shift, 1)[0:1]
                window = jnp.where(lane < 2 * LANES - BP - off, r0, r1)
                last = block_ref[ROWS - 1 : ROWS, :]
                block_ref[ROWS - 1 : ROWS, :] = jnp.where(lane >= LANES - BP, window, last)
                out_ref[owner, pl.ds(pl.multiple_of(rank * ROWS, ROWS), ROWS), :] = block_ref[
                    ...
                ].astype(out_ref.dtype)

            return carry

        lax.fori_loop(0, KMAX, one, 0)


def rest_kernel(
    flow_ref,
    before0_ref,
    after0_ref,
    before1_ref,
    after1_ref,
    base_ref,
    lo0_ref,
    hi0_ref,
    lo1_ref,
    hi1_ref,
    coef_ref,
    axial_ref,
    edge_ref,
    held_ref,
    next_ref,
    ext_ref,
    sems,
):
    del held_ref
    a = pl.program_id(0)
    n = flow_ref.shape[1]
    variables = []
    for var in range(5):
        group = 0 if var in FIRST_AZ else 1
        variables.append((var, (FIRST_AZ, LATER_AZ)[group].index(var), group))
    copies = plane_copies(
        flow_ref, (before0_ref, before1_ref), (after0_ref, after1_ref), ext_ref, sems, variables, n
    )
    feed_planes(a, n, copies)

    def plane(var, offset):
        return ext_ref[var, a + 2 + offset]

    def layers(var):
        if var in FIRST_RAD:
            lo, hi, s = lo0_ref, hi0_ref, FIRST_RAD.index(var)
        else:
            lo, hi, s = lo1_ref, hi1_ref, LATER_RAD.index(var)
        return (
            [lo[s, a, j : j + 1, :] for j in (0, 1)],
            [hi[s, a, j : j + 1, :] for j in (0, 1)],
        )

    for var in range(4):
        next_ref[var, 0] = new_plane(
            var, base_ref[var, 0], plane, layers, coef_ref, axial_ref, edge_ref
        )


def whole(array):
    shape = array.shape
    return pl.BlockSpec(shape, lambda *_: (0,) * len(shape))


def pressure_call(meta, flow, before, after, base, lo, hi, coef, axial, edge, history, owners):
    nvar, planes, rows, length = flow.shape
    one = (1, 1, rows, length)
    any_space = pl.BlockSpec(memory_space=pl.ANY)
    cells = planes * rows * length
    return pl.pallas_call(
        pressure_kernel,
        name="pressure",
        out_shape=(
            jax.ShapeDtypeStruct(flow.shape, jnp.float32),
            jax.ShapeDtypeStruct((owners, CAP * ROWS, LANES), jnp.bfloat16),
        ),
        grid_spec=pltpu.PrefetchScalarGridSpec(
            num_scalar_prefetch=1,
            grid=(planes,),
            in_specs=[
                any_space,
                any_space,
                any_space,
                pl.BlockSpec(one, lambda a, m: (2, a, 0, 0)),
                pl.BlockSpec(one, lambda a, m: (3, a, 0, 0)),
                pl.BlockSpec(one, lambda a, m: (4, a, 0, 0)),
                whole(lo),
                whole(hi),
                whole(coef),
                whole(axial),
                whole(edge),
                whole(history),
            ],
            out_specs=(
                pl.BlockSpec(one, lambda a, m: (4, a, 0, 0)),
                pl.BlockSpec((owners, CAP * ROWS, LANES), lambda a, m: (0, 0, 0)),
            ),
            scratch_shapes=[
                pltpu.VMEM((2, planes + 4, rows, length), jnp.float32),
                pltpu.VMEM((planes, length // LANES, rows, LANES), jnp.float32),
                pltpu.VMEM((ROWS, KMAX, LANES), jnp.float32),
                pltpu.VMEM((ROWS, LANES), jnp.float32),
                pltpu.SMEM((owners,), jnp.int32),
                pltpu.SemaphoreType.DMA((2, planes + 4)),
            ],
        ),
        compiler_params=pltpu.CompilerParams(dimension_semantics=("arbitrary",)),
        cost_estimate=pl.CostEstimate(flops=60 * cells, bytes_accessed=6 * 4 * cells, transcendentals=0),
    )(meta, flow, before, after, flow, flow, base, lo, hi, coef, axial, edge, history)


def rest_call(flow, az0, az1, base, rad0, rad1, coef, axial, edge, held):
    nvar, planes, rows, length = flow.shape
    any_space = pl.BlockSpec(memory_space=pl.ANY)
    cells = planes * rows * length
    four = (4, 1, rows, length)
    args = (flow, *az0, *az1, base, *rad0, *rad1, coef, axial, edge, held)
    return pl.pallas_call(
        rest_kernel,
        name="others",
        out_shape=jax.ShapeDtypeStruct(flow.shape, jnp.float32),
        grid=(planes,),
        in_specs=[
            any_space,
            any_space,
            any_space,
            any_space,
            any_space,
            pl.BlockSpec(four, lambda a: (0, a, 0, 0)),
            *[whole(x) for x in (*rad0, *rad1, coef, axial, edge)],
            any_space,
        ],
        out_specs=pl.BlockSpec(four, lambda a: (0, a, 0, 0)),
        scratch_shapes=[
            pltpu.VMEM((nvar, planes + 4, rows, length), jnp.float32),
            pltpu.SemaphoreType.DMA((nvar, planes + 4)),
        ],
        input_output_aliases={len(args) - 1: 0},
        compiler_params=pltpu.CompilerParams(dimension_semantics=("arbitrary",)),
        cost_estimate=pl.CostEstimate(
            flops=200 * cells, bytes_accessed=13 * 4 * cells, transcendentals=0
        ),
    )(*args)


def weights_kernel(order_ref, stations_ref, weight_ref, out_ref, lhs_ref, packed_ref):
    step = pl.program_id(0)

    @pl.when(step == 0)
    def _():
        for group in range(stations_ref.shape[0] * CAP // QUADS):
            tiles = []
            for m in range(QUADS):
                source, rank = divmod(group * QUADS + m, CAP)
                tile = stations_ref[source, rank * ROWS : (rank + 1) * ROWS, :]
                tiles.append(tile.astype(jnp.float32))
            for i, tile in enumerate(swap_quads(tiles)):
                lhs_ref[i * ROWS : (i + 1) * ROWS, group * LANES : (group + 1) * LANES] = (
                    tile.astype(lhs_ref.dtype)
                )

    part = jnp.dot(lhs_ref[...], weight_ref[...], preferred_element_type=jnp.float32)
    groups = part.shape[1] // LANES
    for group in range(groups):
        lanes = slice(group * LANES, (group + 1) * LANES)
        tiles = [part[i * ROWS : (i + 1) * ROWS, lanes] for i in range(QUADS)]
        for m, tile in enumerate(swap_quads(tiles)):
            packed_ref[(step * groups + group) * QUADS + m] = tile

    @pl.when(step == pl.num_programs(0) - 1)
    def _():
        def move(j, carry):
            out_ref[j] = packed_ref[order_ref[j]]
            return carry

        lax.fori_loop(0, out_ref.shape[0], move, 0, unroll=8)


def weights_call(order, stations, weight):
    count = order.shape[0]
    depth, observers = weight.shape
    tile = 512
    return pl.pallas_call(
        weights_kernel,
        name="observers",
        out_shape=jax.ShapeDtypeStruct((count, ROWS, LANES), jnp.float32),
        grid_spec=pltpu.PrefetchScalarGridSpec(
            num_scalar_prefetch=1,
            grid=(observers // tile,),
            in_specs=[
                pl.BlockSpec(stations.shape, lambda n, o: (0, 0, 0)),
                pl.BlockSpec((depth, tile), lambda n, o: (0, n)),
            ],
            out_specs=pl.BlockSpec((count, ROWS, LANES), lambda n, o: (0, 0, 0)),
            scratch_shapes=[
                pltpu.VMEM((NT, depth), jnp.bfloat16),
                pltpu.VMEM((count, ROWS, LANES), jnp.float32),
            ],
        ),
        compiler_params=pltpu.CompilerParams(dimension_semantics=("arbitrary",)),
        cost_estimate=pl.CostEstimate(
            flops=2 * NT * depth * observers,
            bytes_accessed=2 * depth * observers,
            transcendentals=0,
        ),
    )(order, stations, weight)


def retard_kernel(parts_ref, matrix_ref, out_ref):
    def add(i, total):
        for j in range(8):
            total = total + parts_ref[i * 8 + j]
        return total

    total = lax.fori_loop(
        0, parts_ref.shape[0] // 8, add, jnp.zeros(parts_ref.shape[1:], jnp.float32)
    )
    tall_sum = jnp.concatenate(
        [total if i == 0 else pltpu.roll(total, LANES - i * BP, 1) for i in range(QUADS)], axis=0
    )
    pressure = jnp.dot(
        matrix_ref[...],
        tall_sum,
        precision=lax.Precision.HIGHEST,
        preferred_element_type=jnp.float32,
    )
    lane = lax.broadcasted_iota(jnp.int32, (ROWS, LANES), 1)
    out = pressure[:ROWS]
    for i in range(1, QUADS):
        tile = pltpu.roll(pressure[i * ROWS : (i + 1) * ROWS], i * BP, 1)
        out = jnp.where(lane >= i * BP, tile, out)
    out_ref[...] = out


def retard_call(parts, matrix):
    return pl.pallas_call(
        retard_kernel,
        name="retard",
        out_shape=jax.ShapeDtypeStruct((ROWS, LANES), jnp.float32),
        in_specs=[pl.BlockSpec(memory_space=pltpu.VMEM)] * 2,
        out_specs=pl.BlockSpec(memory_space=pltpu.VMEM),
        cost_estimate=pl.CostEstimate(
            flops=2 * parts.size, bytes_accessed=4 * parts.size, transcendentals=0
        ),
    )(parts, matrix)


def exchange(first, last, axis, wrap):
    count = lax.axis_size(axis)
    up = [(i, (i + 1) % count) for i in range(count if wrap else count - 1)]
    down = [(j, i) for i, j in up]
    return lax.ppermute(last, axis, up), lax.ppermute(first, axis, down)


def azimuth_layers(flow, variables):
    pick = lambda cut: jnp.stack([flow[v, cut] for v in variables])
    return exchange(pick(slice(0, 2)), pick(slice(-2, None)), "azimuth", True)


def radial_layers(flow, variables):
    def pick(cut):
        return jnp.stack([flow[v, :, cut] for v in variables])

    return exchange(pick(slice(0, 2)), pick(slice(-2, None)), "radius", False)


def coefficients(mean_flow, band_index, band_size, cycle_size, planes, rows, length):
    radial_cell = band_index * rows + jnp.arange(rows, dtype=jnp.int32)
    radius_pos = radial_cell.astype(jnp.float32) + (0.5 * rows * band_size + 0.5)
    metric = planes * cycle_size / (2.0 * math.pi) / radius_pos
    dt, nu = SECTION_STEP, VISCOSITY
    turn = mean_flow[0] * metric

    def four(speed):
        return [
            dt * (nu * 16.0 / 12.0 - speed * (8.0 / 12.0)),
            dt * (nu * 16.0 / 12.0 + speed * (8.0 / 12.0)),
            dt * (speed / 12.0 - nu / 12.0),
            -dt * (speed / 12.0 + nu / 12.0),
        ]

    coef = jnp.stack(
        four(turn) + [dt * 8.0 / 12.0 * metric, dt / 12.0 * metric, dt / radius_pos]
    )
    coef = jnp.broadcast_to(coef[:, :, None], (7, rows, LANES))
    z = jnp.arange(length, dtype=jnp.int32)
    inside = jnp.stack([z < length - 1, z >= 1, z < length - 2, z >= 2])
    axial = jnp.where(inside[:, None, :], jnp.stack(four(mean_flow[1]))[:, :, None], 0.0)
    scale = jnp.array([8.0 / 12.0, 8.0 / 12.0, 1.0 / 12.0, 1.0 / 12.0], jnp.float32) * dt
    edge = jnp.where(inside, scale[:, None], 0.0)
    edge = jnp.broadcast_to(edge[:, None, :], (4, 8, length))
    return coef, axial, edge


def per_device(
    flow_state,
    base_state,
    mean_flow,
    panel_history,
    panel_line,
    panel_start,
    panel_count,
    panel_owner,
    source_weight,
    retarded_time,
    observer_block,
):
    cycle_size = lax.axis_size("azimuth")
    band_size = lax.axis_size("radius")
    nvar, planes, rows, length = flow_state.shape
    cycle_index = lax.axis_index("azimuth")
    band_index = lax.axis_index("radius")

    rad0 = radial_layers(flow_state, FIRST_RAD)
    az0 = azimuth_layers(flow_state, FIRST_AZ)
    rad1 = radial_layers(flow_state, LATER_RAD)
    az1 = azimuth_layers(flow_state, LATER_AZ)
    coef, axial, edge = coefficients(
        mean_flow, band_index, band_size, cycle_size, planes, rows, length
    )
    own_owner = lax.dynamic_slice(panel_owner, (cycle_index, band_index, 0), (1, 1, KMAX))[0, 0]
    own_count = lax.dynamic_slice(panel_count, (cycle_index, band_index), (1, 1))[0]
    meta = jnp.concatenate([own_owner, panel_line[0, 0], panel_start[0, 0], own_count])

    held, outgoing = pressure_call(
        meta, flow_state, *az0, base_state, *rad0, coef, axial, edge, panel_history[0, 0], cycle_size
    )
    stations = lax.all_to_all(outgoing, "azimuth", split_axis=0, concat_axis=0, tiled=True)
    sends = weights_call(observer_block, stations, source_weight[0])
    parts = lax.all_to_all(sends, BOTH, split_axis=0, concat_axis=0, tiled=True)
    next_state = rest_call(
        flow_state, az0, az1, base_state, rad0, rad1, coef, axial, edge, held
    )

    chosen = lax.dynamic_index_in_dim(observer_block, lax.axis_index(BOTH), 0, keepdims=False)
    matrix = lax.dynamic_index_in_dim(retarded_time, chosen, 0, keepdims=False)
    matrix = matrix.reshape(ROWS, QUADS, ROWS, QUADS).transpose(1, 0, 3, 2).reshape(NT, NT)
    pressure = retard_call(parts, matrix)
    return next_state, pressure.reshape(1, ROWS * LANES)


def solution(mesh):
    placed = (
        P(None, "azimuth", "radius", None),
        P(None, "azimuth", "radius", None),
        P(None, "radius"),
        P("azimuth", "radius", None, None),
        P("azimuth", "radius", None),
        P("azimuth", "radius", None),
        P(),
        P(),
        P("radius", "azimuth", None),
        P(),
        P(),
    )
    return jax.shard_map(
        per_device,
        mesh=mesh,
        in_specs=placed,
        out_specs=(P(None, "azimuth", "radius", None), P(BOTH, None)),
        check_vma=False,
    )
```

time: 884 us -> 115 us (0.13)
  waiting for transfers between devices: 646 us -> 3.13 us
  local copies, waits for them, and re-layouts: 141 us -> 15.9 us
  other arithmetic: 56.1 us -> 6.67 us
  Pallas kernels: 0 us -> 41.1 us
  blocking collectives: 0 us -> 15.5 us
  between operations: 16.3 us -> 2.84 us
  starting transfers between devices: 15.1 us -> 27.4 us
    reduce_scatter x1 -> x0, waiting for transfers between devices: 642 us -> none  [per_device(): lax.psum_scatter(ordered, ('azimuth', 'radius'), scatter_dimension=1, til...]
    dot_general x3 -> x0, local copies, waits for them, and re-layouts: 66.7 us -> none  [per_device(): jnp.einsum('stp,spo->to', stations.reshape(total_stations, NT, BP), weigh...]
    pallas_call x0 -> x4, Pallas kernels: none -> 41.1 us  [the longest x1 15.5 us: rest_call(): pl.pallas_call(rest_kernel, name='others', out_shape=jax.ShapeDtypeStruct...]
    gather x49 -> x0, local copies, waits for them, and re-layouts: 34.9 us -> none
    unnamed x4 -> x0, other arithmetic: 24 us -> none
    add x1 -> x0, other arithmetic: 20.9 us -> none  [per_device(): base_state + SECTION_STEP * tendency(flow_state, cycle_ext, band_ext, mea...]
    all_to_all x0 -> x1, blocking collectives: none -> 15.5 us  [per_device(): lax.all_to_all(outgoing, 'azimuth', split_axis=0, concat_axis=0, tiled=True)]
    another operation x2 -> x1, local copies, waits for them, and re-layouts: 12.2 us -> 0.02 us  [coefficients(): jnp.stack(four(turn) + [dt * 8.0 / 12.0 * metric, dt / 12.0 * metric, dt...]
  transfers between devices with their start and end apart: 6 -> 9, of which waited for: 2 -> 1; matrix products, arithmetic and copies ran while one was open for 12% -> 16% of each run, Pallas kernels for 0% -> 14%
where the time goes in v1:
time: 115 us; the launch traced here: 113 us
  Pallas kernels  41.1 us (36%)
  starting transfers between devices  27.4 us (24%)
  local copies, waits for them, and re-layouts  15.9 us (14%)
  blocking collectives  15.5 us (13%)
  other arithmetic  6.67 us (6%)
  waiting for transfers between devices  3.13 us (3%)
  between operations  2.84 us (2%)
    ppermute x8, starting transfers between devices, exchange(): return (lax.ppermute(last, axis, up), lax.ppermute(first, axis, down))  20.4 us
    all_to_all x1, blocking collectives, per_device(): lax.all_to_all(outgoing, 'azimuth', split_axis=0, concat_axis=0, tiled=True)  15.5 us
    pallas_call x1, Pallas kernels, rest_call(): pl.pallas_call(rest_kernel, name='others', out_shape=jax.ShapeDtypeStruct...  15.5 us
    pallas_call x1, Pallas kernels, pressure_call(): pl.pallas_call(pressure_kernel, name='pressure', out_shape=(jax.ShapeDtyp...  13.7 us
    pallas_call x1, Pallas kernels, weights_call(): pl.pallas_call(weights_kernel, name='observers', out_shape=jax.ShapeDtype...  9.71 us
    all_to_all x1, starting transfers between devices, per_device(): parts = lax.all_to_all(sends, BOTH, split_axis=0, concat_axis=0, tiled=True)  6.99 us
    slice x2, local copies, waits for them, and re-layouts, pick(): return jnp.stack([flow[v, :, cut] for v in variables])  3.27 us
    ppermute x8, waiting for transfers between devices, exchange(): return (lax.ppermute(last, axis, up), lax.ppermute(first, axis, down))  3.13 us
  transfers between devices with their start and end apart: 9, of which 1 were waited for; matrix products, arithmetic and copies ran while one was open for 16% of the time, Pallas kernels for 14%

profile of v1, /device:TPU:0, one launch (start us, length us, event | category | flops | bytes accessed | tf_op | source)
XLA Modules:
  0.0 112.6 jit_solution(10369387929862116828)
XLA Ops:
  0.6 2.0 %fusion.4 = (f32[1,2,32,384]{3,2,1,0:T(8,128)}, f32[1,2,32,384]{3,2,1,0:T(8,128)}, f32[1,2,32,384]{3,2,1,0:T(8,128)S(1)}, f32[1,2,32,384]{3,2,1,0:T(8,128)S(1)},...) fusion(f32[5,16,32,384]{3,2,1,0:T(8,128)} %flow_ref.3), kind=kLoop, calls=%fused_computation.35 | loop fusion | bytes 1179648 | tf_op jit(solution)/shard_map/slice | solution.py:508
  2.7 6.3 %collective-permute-start.1 = (f32[2,2,32,384]{3,2,1,0:T(8,128)S(1)}, f32[2,2,32,384]{3,2,1,0:T(8,128)S(1)}, u32[]{:S(2)}, u32[]{:S(2)}) collective-permute-start(f32[2,2,32,384]{3,2,1,0:T(8,128)S(1)} %pad_maximum_fusion.3), channel_id=1, source_target_pairs={{8,0},{16,8},{24,16},{32,24},{40,32},{48,40},{56,48},{64,56},{72,6... | collective-permute-start | bytes 589832 | tf_op jit(solution)/shard_map/ppermute | solution.py:504
  9.1 2.1 %fusion.3 = (f32[1,16,2,384]{3,2,1,0:T(2,128)}, f32[1,16,2,384]{3,2,1,0:T(2,128)}, f32[1,16,2,384]{3,2,1,0:T(2,128)S(1)}, f32[1,16,2,384]{3,2,1,0:T(2,128)S(1)},...) fusion(f32[5,16,32,384]{3,2,1,0:T(8,128)} %flow_ref.3), kind=kLoop, calls=%fused_computation.34 | loop fusion | bytes 589824 | tf_op jit(solution)/shard_map/slice | solution.py:514
  11.2 2.6 %collective-permute-start.4 = (f32[2,16,2,384]{3,2,1,0:T(2,128)S(1)}, f32[2,16,2,384]{3,2,1,0:T(2,128)S(1)}, u32[]{:S(2)}, u32[]{:S(2)}) collective-permute-start(f32[2,16,2,384]{3,2,1,0:T(2,128)S(1)} %pad_maximum_fusion.6), channel_id=1, source_target_pairs={{0,1},{1,2},{2,3},{3,4},{4,5},{5,6},{6,7},{8,9},{9,10},{10,11},{11... | collective-permute-start | bytes 294920 | tf_op jit(solution)/shard_map/ppermute | solution.py:504
  13.8 1.3 %collective-permute-start.5 = (f32[2,16,2,384]{3,2,1,0:T(2,128)S(1)}, f32[2,16,2,384]{3,2,1,0:T(2,128)S(1)}, u32[]{:S(2)}, u32[]{:S(2)}) collective-permute-start(f32[2,16,2,384]{3,2,1,0:T(2,128)S(1)} %pad_maximum_fusion.7), channel_id=1, source_target_pairs={{1,0},{2,1},{3,2},{4,3},{5,4},{6,5},{7,6},{9,8},{10,9},{11,10},{12... | collective-permute-start | bytes 294920 | tf_op jit(solution)/shard_map/ppermute | solution.py:504
  17.5 1.3 %dynamic_slice.15 = s32[1,1]{0,1:T(1,128)} dynamic-slice(s32[16,8]{0,1:T(8,128)} %param.18, s32[]{:T(128)S(6)} %select_n.30, s32[]{:T(128)S(6)} %select_n.31), dynamic_slice_sizes={1,1} | dynamic-slice | bytes 12 | tf_op jit(solution)/shard_map/dynamic_slice | solution.py:574
  19.5 2.0 %pad_add_fusion.1.meta_ref = s32[49]{0:T(128)} fusion(s32[1]{0:T(128)} %bitcast.3, s32[16]{0:T(128)} %bitcast.14, s32[16]{0:T(128)} %bitcast.15, s32[16]{0:T(128)S(1)} %dynamic-slice_bitcast_fusion), kind=kLoop, calls=%fused_computation.17 | loop fusion | flops 147 | bytes 392 | tf_op jit(solution)/shard_map/concatenate | solution.py:575
  21.5 0.8 broadcast_in_dim.47.coef_ref
  23.0 13.7 %pressure.1 = (f32[5,16,32,384]{3,2,1,0:T(8,128)}, bf16[16,32,128]{2,1,0:T(8,128)(2,1)}) custom-call(s32[49]{0:T(128)} %pad_add_fusion.1.meta_ref, f32[5,16,32,384]{3,2,1,0:T(8,128)} %flow_ref.3, f32[2,2,32,384]{3,2,1,0:T(8,128)} %copy-done.3, f32[2,2,32,384]{3,2,1,0:T(8,128)} %copy-done.2, f32[5,16,32,384]{3,2,1,0:T(8,128)} %flow_ref.3, ...), custom_call_target="tpu_custom_call" | custom-call | flops 11796480 | bytes 4718592 | tf_op jit(solution)/shard_map/pressure/pallas_call | solution.py:322
  36.6 15.5 %all_to_all.10.stations_ref = bf16[16,32,128]{2,1,0:T(8,128)(2,1)} all-to-all(bf16[16,32,128]{2,1,0:T(8,128)(2,1)} %get-tuple-element.5), channel_id=1, replica_groups=mesh['azimuth'=16,'radius'=8] {'azimuth'}, dimensions={0} | all-to-all | bytes 262144 | tf_op jit(solution)/shard_map/all_to_all | solution.py:580
  52.1 9.7 %observers.1 = f32[128,16,128]{2,1,0:T(8,128)} custom-call(s32[128]{0:T(128)} %order_ref.1, bf16[16,32,128]{2,1,0:T(8,128)(2,1)} %all_to_all.10.stations_ref, bf16[1024,4096]{1,0:T(8,128)(2,1)} %bitcast.10), custom_call_target="tpu_custom_call" | custom-call | flops 536870912 | bytes 8388608 | tf_op jit(solution)/shard_map/observers/pallas_call | solution.py:435
  61.8 7.0 %all-to-all-start.1 = ((f32[128,16,128]{2,1,0:T(8,128)}), f32[128,16,128]{2,1,0:T(8,128)S(1)}, u32[]{:S(2)}, u32[]{:S(2)}) async-start(f32[128,16,128]{2,1,0:T(8,128)} %observers.1), calls=%async_computation.1 | async-start | bytes 2097152 | tf_op jit(solution)/shard_map/all_to_all | solution.py:582
  68.8 1.1 fusion.5
  71.4 5.4 %collective-permute-start.3 = (f32[3,2,32,384]{3,2,1,0:T(8,128)}, f32[3,2,32,384]{3,2,1,0:T(8,128)}, u32[]{:S(2)}, u32[]{:S(2)}) collective-permute-start(f32[3,2,32,384]{3,2,1,0:T(8,128)} %pad_maximum_fusion.1), channel_id=1, source_target_pairs={{8,0},{16,8},{24,16},{32,24},{40,32},{48,40},{56,48},{64,56},{72,6... | collective-permute-start | bytes 884744 | tf_op jit(solution)/shard_map/ppermute | solution.py:504
  76.8 1.2 %fusion.2 = (f32[2,16,2,384]{3,2,1,0:T(2,128)S(1)}, f32[2,16,2,384]{3,2,1,0:T(2,128)S(1)}) fusion(f32[5,16,32,384]{3,2,1,0:T(8,128)} %flow_ref.3), kind=kLoop, calls=%fused_computation.33 | loop fusion | bytes 393216 | tf_op jit(solution)/shard_map/slice | solution.py:514
  78.7 3.5 %collective-permute-start.6 = (f32[3,16,2,384]{3,2,1,0:T(2,128)}, f32[3,16,2,384]{3,2,1,0:T(2,128)}, u32[]{:S(2)}, u32[]{:S(2)}) collective-permute-start(f32[3,16,2,384]{3,2,1,0:T(2,128)} %pad_maximum_fusion.4), channel_id=1, source_target_pairs={{0,1},{1,2},{2,3},{3,4},{4,5},{5,6},{6,7},{8,9},{9,10},{10,11},{11... | collective-permute-start | bytes 442376 | tf_op jit(solution)/shard_map/ppermute | solution.py:504
  82.3 1.3 %collective-permute-start.7 = (f32[3,16,2,384]{3,2,1,0:T(2,128)S(1)}, f32[3,16,2,384]{3,2,1,0:T(2,128)}, u32[]{:S(2)}, u32[]{:S(2)}) collective-permute-start(f32[3,16,2,384]{3,2,1,0:T(2,128)S(1)} %pad_maximum_fusion.5), channel_id=1, source_target_pairs={{1,0},{2,1},{3,2},{4,3},{5,4},{6,5},{7,6},{9,8},{10,9},{11,10},{12... | collective-permute-start | bytes 442376 | tf_op jit(solution)/shard_map/ppermute | solution.py:504
  86.1 1.2 %dynamic-slice_reduce_fusion = f32[64,64]{1,0:T(8,128)S(1)} fusion(f32[128,64,64]{0,2,1:T(8,128)S(1)} %copy-done, s32[]{:T(128)S(6)} %select_n.33), kind=kLoop, calls=%fused_computation | loop fusion | bytes 32772 | tf_op jit(solution)/shard_map/jit(dynamic_index_in_dim)/dynamic_slice | solution.py:588
  87.3 1.1 reshape.112
  88.4 1.5 %copy.15 = f32[4,16,4,16]{3,2,1,0:T(4,128)S(1)} copy(f32[4,16,4,16]{2,3,0,1:T(8,128)} %bitcast.11) | data formatting | bytes 32768 | tf_op jit(solution)/shard_map/transpose | solution.py:589
  90.7 3.1 %collective-permute-done.2.before1_ref = f32[3,2,32,384]{3,2,1,0:T(8,128)} collective-permute-done((f32[3,2,32,384]{3,2,1,0:T(8,128)}, f32[3,2,32,384]{3,2,1,0:T(8,128)}, u32[]{:S(2)}, u32[]{:S(2)}) %collective-permute-start.2) | collective-permute-done | bytes 294944 | tf_op jit(solution)/shard_map/ppermute | solution.py:504
  93.8 15.5 %others.1 = f32[5,16,32,384]{3,2,1,0:T(8,128)} custom-call(f32[5,16,32,384]{3,2,1,0:T(8,128)} %flow_ref.3, f32[2,2,32,384]{3,2,1,0:T(8,128)} %copy-done.3, f32[2,2,32,384]{3,2,1,0:T(8,128)} %copy-done.2, f32[3,2,32,384]{3,2,1,0:T(8,128)} %collective-permute-done.2.before1_ref, ...), custom_call_target="tpu_custom_call", output_to_operand_aliasing={{}: (13, {})} | custom-call | flops 39321600 | bytes 10223616 | tf_op jit(solution)/shard_map/others/pallas_call | solution.py:370
  109.3 1.0 copy-done.1
  110.3 2.3 %retard.1 = f32[16,128]{1,0:T(8,128)} custom-call(f32[128,16,128]{2,1,0:T(8,128)} %copy-done.1, f32[64,64]{1,0:T(8,128)} %reshape.113.matrix_ref), custom_call_target="tpu_custom_call" | custom-call | flops 524288 | bytes 1048576 | tf_op jit(solution)/shard_map/retard/pallas_call | solution.py:488
  (52 shorter events, 7.5 us)
Async XLA Ops:
  0.6 85.5 %copy-start = (f32[128,64,64]{0,2,1:T(8,128)S(1)}, f32[128,64,64]{0,2,1:T(8,128)}, u32[]{:S(2)}) copy-start(f32[128,64,64]{0,2,1:T(8,128)} %param.21) | copy-start | bytes 6291460
  2.7 18.8 %collective-permute-start.1 = (f32[2,2,32,384]{3,2,1,0:T(8,128)S(1)}, f32[2,2,32,384]{3,2,1,0:T(8,128)S(1)}, u32[]{:S(2)}, u32[]{:S(2)}) collective-permute-start(f32[2,2,32,384]{3,2,1,0:T(8,128)S(1)} %pad_maximum_fusion.3), channel_id=1, source_target_pairs={{8,0},{16,8},{24,16},{32,24},{40,32},{48,40},{56,48},{64,56},{72,6... | collective-permute-start | bytes 589832 | tf_op jit(solution)/shard_map/ppermute | solution.py:504
  9.0 12.5 %collective-permute-start = (f32[2,2,32,384]{3,2,1,0:T(8,128)S(1)}, f32[2,2,32,384]{3,2,1,0:T(8,128)S(1)}, u32[]{:S(2)}, u32[]{:S(2)}) collective-permute-start(f32[2,2,32,384]{3,2,1,0:T(8,128)S(1)} %pad_maximum_fusion.2), channel_id=1, source_target_pairs={{0,8},{8,16},{16,24},{24,32},{32,40},{40,48},{48,56},{56,64},{64,7... | collective-permute-start | bytes 589832 | tf_op jit(solution)/shard_map/ppermute | solution.py:504
  11.2 10.3 %collective-permute-start.4 = (f32[2,16,2,384]{3,2,1,0:T(2,128)S(1)}, f32[2,16,2,384]{3,2,1,0:T(2,128)S(1)}, u32[]{:S(2)}, u32[]{:S(2)}) collective-permute-start(f32[2,16,2,384]{3,2,1,0:T(2,128)S(1)} %pad_maximum_fusion.6), channel_id=1, source_target_pairs={{0,1},{1,2},{2,3},{3,4},{4,5},{5,6},{6,7},{8,9},{9,10},{10,11},{11... | collective-permute-start | bytes 294920 | tf_op jit(solution)/shard_map/ppermute | solution.py:504
  13.8 7.6 %collective-permute-start.5 = (f32[2,16,2,384]{3,2,1,0:T(2,128)S(1)}, f32[2,16,2,384]{3,2,1,0:T(2,128)S(1)}, u32[]{:S(2)}, u32[]{:S(2)}) collective-permute-start(f32[2,16,2,384]{3,2,1,0:T(2,128)S(1)} %pad_maximum_fusion.7), channel_id=1, source_target_pairs={{1,0},{2,1},{3,2},{4,3},{5,4},{6,5},{7,6},{9,8},{10,9},{11,10},{12... | collective-permute-start | bytes 294920 | tf_op jit(solution)/shard_map/ppermute | solution.py:504
  21.4 1.5 %copy-start.4 = (f32[2,16,2,384]{3,2,1,0:T(2,128)}, f32[2,16,2,384]{3,2,1,0:T(2,128)S(1)}, u32[]{:S(2)}) copy-start(f32[2,16,2,384]{3,2,1,0:T(2,128)S(1)} %collective-permute-done.4.lo_ref.lo0_ref) | copy-start | bytes 294916
  21.5 1.5 %copy-start.5 = (f32[2,16,2,384]{3,2,1,0:T(2,128)}, f32[2,16,2,384]{3,2,1,0:T(2,128)S(1)}, u32[]{:S(2)}) copy-start(f32[2,16,2,384]{3,2,1,0:T(2,128)S(1)} %collective-permute-done.5.hi_ref.hi0_ref) | copy-start | bytes 294916
  21.5 1.5 %copy-start.2 = (f32[2,2,32,384]{3,2,1,0:T(8,128)}, f32[2,2,32,384]{3,2,1,0:T(8,128)S(1)}, u32[]{:S(2)}) copy-start(f32[2,2,32,384]{3,2,1,0:T(8,128)S(1)} %collective-permute-done.1.after_ref.after0_ref) | copy-start | bytes 589828
  21.5 1.5 %copy-start.3 = (f32[2,2,32,384]{3,2,1,0:T(8,128)}, f32[2,2,32,384]{3,2,1,0:T(8,128)S(1)}, u32[]{:S(2)}) copy-start(f32[2,2,32,384]{3,2,1,0:T(8,128)S(1)} %collective-permute-done.before_ref.before0_ref) | copy-start | bytes 589828
  52.1 17.8 %copy-start.7 = (f32[1,2,32,384]{3,2,1,0:T(8,128)S(1)}, f32[1,2,32,384]{3,2,1,0:T(8,128)}, u32[]{:S(2)}) copy-start(f32[1,2,32,384]{3,2,1,0:T(8,128)} %get-tuple-element.19) | copy-start | bytes 294916
  52.1 18.5 %copy-start.6 = (f32[1,2,32,384]{3,2,1,0:T(8,128)S(1)}, f32[1,2,32,384]{3,2,1,0:T(8,128)}, u32[]{:S(2)}) copy-start(f32[1,2,32,384]{3,2,1,0:T(8,128)} %get-tuple-element.18) | copy-start | bytes 294916
  61.8 16.1 %copy-start.9 = (f32[1,16,2,384]{3,2,1,0:T(2,128)S(1)}, f32[1,16,2,384]{3,2,1,0:T(2,128)}, u32[]{:S(2)}) copy-start(f32[1,16,2,384]{3,2,1,0:T(2,128)} %get-tuple-element.13) | copy-start | bytes 147460
  61.8 20.4 %copy-start.8 = (f32[1,16,2,384]{3,2,1,0:T(2,128)S(1)}, f32[1,16,2,384]{3,2,1,0:T(2,128)}, u32[]{:S(2)}) copy-start(f32[1,16,2,384]{3,2,1,0:T(2,128)} %get-tuple-element.12) | copy-start | bytes 147460
  61.8 21.8 %copy-start.10 = (s32[128]{0:T(128)S(1)}, s32[128]{0:T(128)}, u32[]{:S(2)}) copy-start(s32[128]{0:T(128)} %order_ref.1) | copy-start | bytes 1540
  61.8 47.4 %all-to-all-start.1 = ((f32[128,16,128]{2,1,0:T(8,128)}), f32[128,16,128]{2,1,0:T(8,128)S(1)}, u32[]{:S(2)}, u32[]{:S(2)}) async-start(f32[128,16,128]{2,1,0:T(8,128)} %observers.1), calls=%async_computation.1 | async-start | bytes 2097152 | tf_op jit(solution)/shard_map/all_to_all | solution.py:582
  70.6 23.1 %collective-permute-start.2 = (f32[3,2,32,384]{3,2,1,0:T(8,128)}, f32[3,2,32,384]{3,2,1,0:T(8,128)}, u32[]{:S(2)}, u32[]{:S(2)}) collective-permute-start(f32[3,2,32,384]{3,2,1,0:T(8,128)} %pad_maximum_fusion), channel_id=1, source_target_pairs={{0,8},{8,16},{16,24},{24,32},{32,40},{40,48},{48,56},{56,64},{64,7... | collective-permute-start | bytes 884744 | tf_op jit(solution)/shard_map/ppermute | solution.py:504
  71.4 22.4 %collective-permute-start.3 = (f32[3,2,32,384]{3,2,1,0:T(8,128)}, f32[3,2,32,384]{3,2,1,0:T(8,128)}, u32[]{:S(2)}, u32[]{:S(2)}) collective-permute-start(f32[3,2,32,384]{3,2,1,0:T(8,128)} %pad_maximum_fusion.1), channel_id=1, source_target_pairs={{8,0},{16,8},{24,16},{32,24},{40,32},{48,40},{56,48},{64,56},{72,6... | collective-permute-start | bytes 884744 | tf_op jit(solution)/shard_map/ppermute | solution.py:504
  78.7 12.0 %collective-permute-start.6 = (f32[3,16,2,384]{3,2,1,0:T(2,128)}, f32[3,16,2,384]{3,2,1,0:T(2,128)}, u32[]{:S(2)}, u32[]{:S(2)}) collective-permute-start(f32[3,16,2,384]{3,2,1,0:T(2,128)} %pad_maximum_fusion.4), channel_id=1, source_target_pairs={{0,1},{1,2},{2,3},{3,4},{4,5},{5,6},{6,7},{8,9},{9,10},{10,11},{11... | collective-permute-start | bytes 442376 | tf_op jit(solution)/shard_map/ppermute | solution.py:504
  82.3 8.4 %collective-permute-start.7 = (f32[3,16,2,384]{3,2,1,0:T(2,128)S(1)}, f32[3,16,2,384]{3,2,1,0:T(2,128)}, u32[]{:S(2)}, u32[]{:S(2)}) collective-permute-start(f32[3,16,2,384]{3,2,1,0:T(2,128)S(1)} %pad_maximum_fusion.5), channel_id=1, source_target_pairs={{1,0},{2,1},{3,2},{4,3},{5,4},{6,5},{7,6},{9,8},{10,9},{11,10},{12... | collective-permute-start | bytes 442376 | tf_op jit(solution)/shard_map/ppermute | solution.py:504
  109.3 1.0 copy-start.1

commit v2 on v0

v2 whole, which is shorter than its diff:
```python
import functools
import math

import jax
import jax.numpy as jnp
from jax import lax
from jax.experimental import pallas as pl
from jax.experimental.pallas import tpu as pltpu
from jax.sharding import PartitionSpec as P

NT = 64
BP = 32
KMAX = 16
CAP = 2
LANES = 128
ROWS = NT * BP // LANES
QUADS = LANES // BP

SECTION_STEP = 0.3
VISCOSITY = 0.05
BOTH = ("azimuth", "radius")

NVAR = 5
FIRST_AZ = (1, 4)
FIRST_RAD = (2, 4)
LATER_AZ = (0, 2, 3)
LATER_RAD = (0, 1, 3)


def swap_quads(tiles):
    lane = lax.broadcasted_iota(jnp.int32, tiles[0].shape, 1)
    low, even = (lane % 128) < 64, (lane % 64) < 32
    a0, a1, a2, a3 = tiles

    def turn(x, shift):
        return pltpu.roll(x, shift, 1)

    b0 = jnp.where(low, a0, turn(a2, 64))
    b2 = jnp.where(low, turn(a0, 64), a2)
    b1 = jnp.where(low, a1, turn(a3, 64))
    b3 = jnp.where(low, turn(a1, 64), a3)
    return (
        jnp.where(even, b0, turn(b1, 32)),
        jnp.where(even, turn(b0, 96), b1),
        jnp.where(even, b2, turn(b3, 32)),
        jnp.where(even, turn(b2, 96), b3),
    )


ORDER = FIRST_AZ + LATER_AZ
EDGE = 8
CHUNK = 4


def plane_copies(flow_ref, before_refs, after_refs, ext_ref, sems):
    planes, rows, length = flow_ref.shape[1:]
    stages = []

    def put(src, place, spots, t, stage):
        dst = ext_ref.at[place, spots, t, pl.ds(EDGE, rows)]
        stages[-1].append(pltpu.make_async_copy(src, dst, sems.at[stage, place, t]))

    def layers(refs, spot, stage):
        place = 0
        for ref in refs:
            for s in range(ref.shape[0]):
                for t in range(length // LANES):
                    src = ref.at[s, :, :, pl.ds(t * LANES, LANES)]
                    put(src, place, pl.ds(spot, 2), t, stage)
                place += 1

    stages.append([])
    layers(before_refs, 0, 0)
    for c in range(planes // CHUNK):
        stages.append([])
        for place, var in enumerate(ORDER):
            for t in range(length // LANES):
                at = pl.ds(c * CHUNK, CHUNK)
                src = flow_ref.at[var, at, :, pl.ds(t * LANES, LANES)]
                put(src, place, pl.ds(c * CHUNK + 2, CHUNK), t, c + 1)
    stages.append([])
    layers(after_refs, planes + 2, planes // CHUNK + 1)
    return stages


def feed_planes(a, stages):
    @pl.when(a == 0)
    def _():
        for stage in stages:
            for c in stage:
                c.start()
        for c in stages[0] + stages[1]:
            c.wait()

    for i, stage in enumerate(stages[2:]):

        @pl.when(a == (i + 1) * CHUNK - 2)
        def _():
            for c in stage:
                c.wait()


def axial_shifts(tiles):
    lane = lax.broadcasted_iota(jnp.int32, tiles[0].shape, 1)
    count = len(tiles)
    shifts = []
    for offset in (1, -1, 2, -2):
        turned = [pltpu.roll(t, (-offset) % LANES, 1) for t in tiles]
        step = 1 if offset > 0 else -1
        outside = lane >= LANES - offset if offset > 0 else lane < -offset
        shifts.append(
            [
                jnp.where(outside, turned[t + step] if 0 <= t + step < count else 0.0, turned[t])
                for t in range(count)
            ]
        )
    return [tuple(s[t] for s in shifts) for t in range(count)]


def plane_update(part, coef, base):
    k8, k1 = SECTION_STEP * 8.0 / 12.0, SECTION_STEP / 12.0
    r1, r2 = SECTION_STEP * VISCOSITY * 16.0 / 12.0, SECTION_STEP * VISCOSITY / 12.0
    c0 = -3.0 * 30.0 / 12.0 * SECTION_STEP * VISCOSITY

    def slope(far, near, p1, m1, p2, m2):
        return near * (p1 - m1) - far * (p2 - m2)

    totals = {}
    extra = {}
    for var in (4, 2, 3, 1, 0):
        centre = part(var, 0, 0)
        axial = axial_shifts(centre)
        cycle = list(zip(*[part(var, d, 0) for d in (1, -1, 2, -2)]))
        band = list(zip(*[part(var, 0, d) for d in (1, -1, 2, -2)]))
        values = base(var)
        totals[var] = []
        for t, x in enumerate(centre):
            total = values[t] + c0 * x
            for i in range(4):
                total += coef(i) * cycle[t][i]
                total += coef(7 + i) * axial[t][i]
            total += r1 * (band[t][0] + band[t][1])
            total -= r2 * (band[t][2] + band[t][3])
            if var == 4:
                extra[1, t] = slope(coef(5), coef(4), *cycle[t])
                extra[2, t] = slope(k1, k8, *band[t])
                extra[3, t] = slope(k1, k8, *axial[t])
            elif var == 2:
                extra[0, t] = slope(k1, k8, *band[t]) + coef(6) * x
            elif var == 3:
                extra[0, t] += slope(k1, k8, *axial[t])
            elif var == 1:
                extra[0, t] += slope(coef(5), coef(4), *cycle[t])
            if var in (1, 2, 3, 0):
                total -= extra[var, t]
            totals[var].append(total)
    for t in range(len(totals[4])):
        totals[4][t] -= extra[0, t]
    return totals


def pack_kernel(flow_ref, az_first_ref, az_last_ref, rad_first_ref, rad_last_ref, edge_ref, sems, *, az, rad):
    planes, rows = flow_ref.shape[1:3]
    direct, edges = [], []
    for s, var in enumerate(rad):
        for side, start in enumerate((0, rows - 8)):
            edges.append(
                pltpu.make_async_copy(
                    flow_ref.at[var, :, pl.ds(start, 8)], edge_ref.at[side, s], sems.at[1, side, s]
                )
            )
    for s, var in enumerate(az):
        for side, (ref, start) in enumerate(((az_first_ref, 0), (az_last_ref, planes - 2))):
            direct.append(
                pltpu.make_async_copy(
                    flow_ref.at[var, pl.ds(start, 2)], ref.at[s], sems.at[0, side, s]
                )
            )
    for c in edges + direct:
        c.start()
    for c in edges:
        c.wait()
    for a in range(planes):
        for s in range(len(rad)):
            rad_first_ref[a, 2 * s : 2 * s + 2, :] = edge_ref[0, s, a, 0:2, :]
            rad_last_ref[a, 2 * s : 2 * s + 2, :] = edge_ref[1, s, a, 6:8, :]
    for c in direct:
        c.wait()


def slots_of(count_ref):
    cycle, band = lax.axis_index("azimuth"), lax.axis_index("radius")
    return cycle, band, count_ref[band, cycle]


def for_live_slots(owner_ref, count_ref, rank_ref, visit):
    cycle, band, count = slots_of(count_ref)
    for q in range(rank_ref.shape[0]):
        rank_ref[q] = 0

    def one(k, carry):
        owner = owner_ref[cycle, band, k]
        rank = rank_ref[owner]
        rank_ref[owner] = rank + 1
        visit(k, owner, rank)
        return carry

    lax.fori_loop(0, count, one, 0)


def fill_coefficients(coef_ref, mean_ref, planes):
    rows = coef_ref.shape[1]
    dt, nu = SECTION_STEP, VISCOSITY
    eye = lax.broadcasted_iota(jnp.int32, (rows, rows), 0) == lax.broadcasted_iota(
        jnp.int32, (rows, rows), 1
    )

    def column(i):
        spread = jnp.where(eye, mean_ref[i : i + 1, :], 0.0)
        return jnp.broadcast_to(jnp.sum(spread, axis=1, keepdims=True), (rows, LANES))

    cell = lax.broadcasted_iota(jnp.int32, (rows, LANES), 0) + lax.axis_index("radius") * rows
    radius_pos = cell.astype(jnp.float32) + (0.5 * rows * lax.axis_size("radius") + 0.5)
    metric = planes * lax.axis_size("azimuth") / (2.0 * math.pi) / radius_pos
    turn = column(0) * metric
    for at, speed in ((0, turn), (7, column(1))):
        coef_ref[at] = dt * (nu * 16.0 / 12.0 - speed * (8.0 / 12.0))
        coef_ref[at + 1] = dt * (nu * 16.0 / 12.0 + speed * (8.0 / 12.0))
        coef_ref[at + 2] = dt * (speed / 12.0 - nu / 12.0)
        coef_ref[at + 3] = -dt * (speed / 12.0 + nu / 12.0)
    coef_ref[4] = dt * 8.0 / 12.0 * metric
    coef_ref[5] = dt / 12.0 * metric
    coef_ref[6] = dt / radius_pos


def panels_kernel(
    owner_ref,
    count_ref,
    line_ref,
    mean_ref,
    flow_ref,
    base_ref,
    history_ref,
    out_ref,
    rows_ref,
    coef_ref,
    store_ref,
    wide_ref,
    block_ref,
    rank_ref,
    sems,
):
    planes, tiles, band = store_ref.shape[1:4]
    sources = ((flow_ref, 4), (flow_ref, 1), (flow_ref, 2), (flow_ref, 3), (base_ref, 4))
    copies = [
        pltpu.make_async_copy(
            ref.at[var, :, :, pl.ds(t * LANES, LANES)], store_ref.at[s, :, t], sems.at[s, t]
        )
        for s, (ref, var) in enumerate(sources)
        for t in range(tiles)
    ]
    for c in copies:
        c.start()
    fill_coefficients(coef_ref, mean_ref, planes)
    wide_ref[ROWS - 1] = jnp.zeros_like(wide_ref[ROWS - 1])
    for r in range(ROWS):
        width = min(LANES, history_ref.shape[1] - r * LANES)
        chunk = history_ref[:, r * LANES : r * LANES + width]
        wide_ref[r, :, 0:width] = chunk.astype(jnp.float32)
    out_ref[...] = jnp.zeros_like(out_ref)

    def place(k, owner, rank):
        for r in range(ROWS):
            block_ref[r : r + 1, :] = wide_ref[r, pl.ds(k, 1), :]
        at = pl.ds(pl.multiple_of(rank * ROWS, ROWS), ROWS)
        out_ref[owner, at, :] = block_ref[...].astype(out_ref.dtype)

    for_live_slots(owner_ref, count_ref, rank_ref, place)
    for c in copies:
        c.wait()

    lane = lax.broadcasted_iota(jnp.int32, (1, LANES), 1)
    k8, k1 = SECTION_STEP * 8.0 / 12.0, SECTION_STEP / 12.0
    r1, r2 = SECTION_STEP * VISCOSITY * 16.0 / 12.0, SECTION_STEP * VISCOSITY / 12.0

    def shifted(x, offset):
        turned = [pltpu.roll(t, (-offset) % LANES, 1) for t in x]
        zero = jnp.zeros_like(x[0])
        if offset < 0:
            return [
                jnp.where(lane < -offset, turned[t - 1] if t else zero, turned[t])
                for t in range(tiles)
            ]
        return [
            jnp.where(lane >= LANES - offset, turned[t + 1] if t + 1 < tiles else zero, turned[t])
            for t in range(tiles)
        ]

    def local(k, carry):
        line = line_ref[0, 0, k]
        la, lr = lax.div(line, band), lax.rem(line, band)

        def row(s, a, r):
            return [store_ref[s, a, t, pl.ds(r, 1), :] for t in range(tiles)]

        def coef(i, inside=None):
            value = coef_ref[i, pl.ds(lr, 1), :]
            return value if inside is None else jnp.where(inside, value, 0.0)

        center = row(0, la, lr)
        total = row(4, la, lr)

        def add(share, x):
            for t in range(tiles):
                total[t] = total[t] + share * x[t]

        add(-3.0 * 30.0 / 12.0 * SECTION_STEP * VISCOSITY, center)
        add(-coef(6), row(2, la, lr))
        turn = {1: -1.0, -1: 1.0, 2: 1.0, -2: -1.0}
        wind = row(3, la, lr)
        for i, offset in enumerate((1, -1, 2, -2)):
            far = abs(offset) == 2
            plane = la + offset
            inside = jnp.logical_and(plane >= 0, plane < planes)
            plane = jnp.clip(plane, 0, planes - 1)
            add(coef(i, inside), row(0, plane, lr))
            add(turn[offset] * coef(5 if far else 4, inside), row(1, plane, lr))
            cell = lr + offset
            inside = jnp.logical_and(cell >= 0, cell < band)
            cell = jnp.clip(cell, 0, band - 1)
            add(jnp.where(inside, -r2 if far else r1, 0.0), row(0, la, cell))
            add(jnp.where(inside, turn[offset] * (k1 if far else k8), 0.0), row(2, la, cell))
            add(coef(7 + i), shifted(center, offset))
            add(turn[offset] * (k1 if far else k8), shifted(wind, offset))
        for t in range(tiles):
            rows_ref[k, t : t + 1, :] = total[t]
        return carry

    lax.fori_loop(0, slots_of(count_ref)[2], local, 0)


def fresh_kernel(
    owner_ref,
    count_ref,
    line_ref,
    start_ref,
    coef_ref,
    rows_ref,
    before_ref,
    after_ref,
    lo_ref,
    hi_ref,
    held_ref,
    out_ref,
    ring_ref,
    sum_ref,
    rank_ref,
):
    tiles, band = ring_ref.shape[1:3]
    planes = lo_ref.shape[0]
    for s in range(2):
        for side, ref in enumerate((before_ref, after_ref)):
            for j in range(2):
                for t in range(tiles):
                    ring_ref[4 * s + 2 * side + j, t] = ref[s, j, :, t * LANES : (t + 1) * LANES]
    out_ref[...] = held_ref[...]
    lane = lax.broadcasted_iota(jnp.int32, (ROWS, LANES), 1)
    row_of = lax.broadcasted_iota(jnp.int32, (ROWS, LANES), 0)
    k8, k1 = SECTION_STEP * 8.0 / 12.0, SECTION_STEP / 12.0
    r1, r2 = SECTION_STEP * VISCOSITY * 16.0 / 12.0, SECTION_STEP * VISCOSITY / 12.0

    def shares(spot, count, near_before, far_before, near_after, far_after):
        first, second = spot == 0, spot == 1
        last, other = spot == count - 1, spot == count - 2
        return (
            jnp.where(first, far_before, 0.0),
            jnp.where(first, near_before, jnp.where(second, far_before, 0.0)),
            jnp.where(last, near_after, jnp.where(other, far_after, 0.0)),
            jnp.where(last, far_after, 0.0),
        )

    def put(k, owner, rank):
        line, start = line_ref[0, 0, k], start_ref[0, 0, k]
        la, lr = lax.div(line, band), lax.rem(line, band)
        for t in range(tiles):
            sum_ref[t : t + 1, :] = rows_ref[k, t : t + 1, :]

        @pl.when(jnp.logical_or(la < 2, la >= planes - 2))
        def _():
            c = [coef_ref[i, pl.ds(lr, 1), :] for i in range(6)]
            wind = shares(la, planes, c[4], -c[5], -c[4], c[5])
            own = shares(la, planes, c[1], c[3], c[0], c[2])
            for t in range(tiles):
                total = sum_ref[t : t + 1, :]
                for j in range(4):
                    total += wind[j] * ring_ref[j, t, pl.ds(lr, 1), :]
                    total += own[j] * ring_ref[4 + j, t, pl.ds(lr, 1), :]
                sum_ref[t : t + 1, :] = total

        @pl.when(jnp.logical_or(lr < 2, lr >= band - 2))
        def _():
            wind = shares(lr, band, k8, -k1, -k8, k1)
            own = shares(lr, band, r1, -r2, r1, -r2)
            for t in range(tiles):
                at = slice(t * LANES, (t + 1) * LANES)
                total = sum_ref[t : t + 1, :]
                for j in range(4):
                    ref = lo_ref if j < 2 else hi_ref
                    total += wind[j] * ref[la, j % 2 : j % 2 + 1, at]
                    total += own[j] * ref[la, 2 + j % 2 : 3 + j % 2, at]
                sum_ref[t : t + 1, :] = total

        tile, off = lax.div(start, LANES), lax.rem(start, LANES)
        other = jnp.minimum(tile + 1, tiles - 1)
        shift = lax.rem(2 * LANES - BP - off, LANES)
        x0 = jnp.broadcast_to(sum_ref[pl.ds(tile, 1), :], (ROWS, LANES))
        x1 = jnp.broadcast_to(sum_ref[pl.ds(other, 1), :], (ROWS, LANES))
        window = jnp.where(
            lane < 2 * LANES - BP - off, pltpu.roll(x0, shift, 1), pltpu.roll(x1, shift, 1)
        )
        at = pl.ds(pl.multiple_of(rank * ROWS, ROWS), ROWS)
        block = out_ref[owner, at, :].astype(jnp.float32)
        place = jnp.logical_and(row_of == ROWS - 1, lane >= LANES - BP)
        out_ref[owner, at, :] = jnp.where(place, window, block).astype(out_ref.dtype)

    for_live_slots(owner_ref, count_ref, rank_ref, put)


def fields_kernel(
    flow_ref,
    before0_ref,
    after0_ref,
    before1_ref,
    after1_ref,
    base_ref,
    lo0_ref,
    hi0_ref,
    lo1_ref,
    hi1_ref,
    coef_ref,
    next_ref,
    ext_ref,
    sems,
):
    a = pl.program_id(0)
    rows, length = flow_ref.shape[2:]
    tiles = length // LANES
    stages = plane_copies(
        flow_ref, (before0_ref, before1_ref), (after0_ref, after1_ref), ext_ref, sems
    )
    feed_planes(a, stages)
    for var in range(NVAR):
        if var in FIRST_RAD:
            lo, hi, s = lo0_ref, hi0_ref, FIRST_RAD.index(var)
        else:
            lo, hi, s = lo1_ref, hi1_ref, LATER_RAD.index(var)
        for t in range(tiles):
            lanes = slice(t * LANES, (t + 1) * LANES)
            place = ORDER.index(var)
            ext_ref[place, a + 2, t, EDGE - 2 : EDGE, :] = lo[a, 2 * s : 2 * s + 2, lanes]
            ext_ref[place, a + 2, t, EDGE + rows : EDGE + rows + 2, :] = hi[
                a, 2 * s : 2 * s + 2, lanes
            ]

    half = 16
    for start in range(0, rows, half):
        at = slice(start, start + half)

        def part(var, offset, row_shift):
            first = EDGE + start + row_shift
            return [
                ext_ref[ORDER.index(var), a + 2 + offset, t, first : first + half, :]
                for t in range(tiles)
            ]

        def coef(i):
            return coef_ref[i, at, :]

        def base(var):
            return [base_ref[var, 0, at, t * LANES : (t + 1) * LANES] for t in range(tiles)]

        totals = plane_update(part, coef, base)
        for var in range(NVAR):
            for t in range(tiles):
                next_ref[var, 0, at, t * LANES : (t + 1) * LANES] = totals[var][t]


ANY = pl.BlockSpec(memory_space=pltpu.HBM)
IN_SMEM = pl.BlockSpec(memory_space=pltpu.SMEM)
IN_VMEM = pl.BlockSpec(memory_space=pltpu.VMEM)
MIB = 1 << 20


def limits(mib, **more):
    return pltpu.CompilerParams(vmem_limit_bytes=mib * MIB, **more)


def cost(flops, moved):
    return pl.CostEstimate(flops=flops, bytes_accessed=moved, transcendentals=0)


def in_hbm(array):
    return pltpu.with_memory_space_constraint(array, pltpu.HBM)


def whole(array):
    shape = array.shape
    return pl.BlockSpec(shape, lambda *_: (0,) * len(shape))


def pack_call(flow, az, rad):
    _, planes, rows, length = flow.shape
    az_shape = jax.ShapeDtypeStruct((len(az), 2, rows, length), jnp.float32)
    rad_shape = jax.ShapeDtypeStruct((planes, 2 * len(rad), length), jnp.float32)
    return pl.pallas_call(
        functools.partial(pack_kernel, az=az, rad=rad),
        out_shape=(az_shape, az_shape, rad_shape, rad_shape),
        in_specs=[ANY],
        out_specs=(IN_VMEM,) * 4,
        scratch_shapes=[
            pltpu.VMEM((2, len(rad), planes, 8, length), jnp.float32),
            pltpu.SemaphoreType.DMA((2, 2, max(len(az), len(rad)))),
        ],
        compiler_params=limits(8),
        cost_estimate=cost(0, 8 * len(az) * 4 * rows * length),
    )(in_hbm(flow))


def panels_call(owner, count, line, mean_flow, flow, base, history):
    _, planes, rows, length = flow.shape
    owners, tiles = count.shape[1], length // LANES
    return pl.pallas_call(
        panels_kernel,
        name="panels",
        out_shape=(
            jax.ShapeDtypeStruct((owners, CAP * ROWS, LANES), jnp.bfloat16),
            jax.ShapeDtypeStruct((KMAX, 8, LANES), jnp.float32),
            jax.ShapeDtypeStruct((11, rows, LANES), jnp.float32),
        ),
        in_specs=[IN_SMEM] * 3 + [IN_VMEM, ANY, ANY, IN_VMEM],
        out_specs=(IN_VMEM,) * 3,
        scratch_shapes=[
            pltpu.VMEM((5, planes, tiles, rows, LANES), jnp.float32),
            pltpu.VMEM((ROWS, KMAX, LANES), jnp.float32),
            pltpu.VMEM((ROWS, LANES), jnp.float32),
            pltpu.SMEM((owners,), jnp.int32),
            pltpu.SemaphoreType.DMA((5, tiles)),
        ],
        compiler_params=limits(8),
        cost_estimate=cost(0, 5 * 4 * planes * rows * length),
    )(owner, count, line, mean_flow, in_hbm(flow), in_hbm(base), history)


def fresh_call(owner, count, line, start, coef, rows, az, rad, held):
    length = az[0].shape[-1]
    band = az[0].shape[2]
    return pl.pallas_call(
        fresh_kernel,
        name="fresh",
        out_shape=jax.ShapeDtypeStruct(held.shape, held.dtype),
        in_specs=[IN_SMEM] * 4 + [IN_VMEM] * 7,
        out_specs=IN_VMEM,
        scratch_shapes=[
            pltpu.VMEM((8, length // LANES, band, LANES), jnp.float32),
            pltpu.VMEM((8, LANES), jnp.float32),
            pltpu.SMEM((held.shape[0],), jnp.int32),
        ],
        compiler_params=limits(8),
        cost_estimate=cost(0, 4 * 4 * band * length * 4),
    )(owner, count, line, start, coef, rows, *az, *rad, held)


def fields_call(flow, az0, az1, base, rad0, rad1, coef):
    nvar, planes, rows, length = flow.shape
    cells = planes * rows * length
    every = (nvar, 1, rows, length)
    args = (in_hbm(flow), *az0, *az1, in_hbm(base), *rad0, *rad1, coef)
    return pl.pallas_call(
        fields_kernel,
        name="fields",
        out_shape=jax.ShapeDtypeStruct(flow.shape, jnp.float32),
        grid=(planes,),
        in_specs=[
            *[ANY] + [pl.BlockSpec(memory_space=pl.ANY)] * 4,
            pl.BlockSpec(every, lambda a: (0, a, 0, 0)),
            *[whole(x) for x in (*rad0, *rad1, coef)],
        ],
        out_specs=pl.BlockSpec(every, lambda a: (0, a, 0, 0)),
        scratch_shapes=[
            pltpu.VMEM(
                (nvar, planes + 4, length // LANES, rows + 2 * EDGE, LANES), jnp.float32
            ),
            pltpu.SemaphoreType.DMA((planes // CHUNK + 2, nvar, length // LANES)),
        ],
        compiler_params=limits(14, dimension_semantics=("arbitrary",)),
        cost_estimate=cost(250 * cells, 15 * 4 * cells),
    )(*args)


def weights_kernel(
    order_ref, stations_ref, weight_ref, out_ref, lhs_ref, held_ref, spot_ref, sems
):
    chunks, _, width = held_ref.shape

    def copy(i):
        at = pl.ds(pl.multiple_of(i * width, width), width)
        return pltpu.make_async_copy(weight_ref.at[:, at], held_ref.at[i], sems.at[i])

    for i in range(chunks):
        copy(i).start()

    def place(j, carry):
        spot_ref[order_ref[j]] = j
        return carry

    lax.fori_loop(0, out_ref.shape[0], place, 0, unroll=8)
    for group in range(stations_ref.shape[0] * CAP // QUADS):
        tiles = []
        for m in range(QUADS):
            source, rank = divmod(group * QUADS + m, CAP)
            tile = stations_ref[source, rank * ROWS : (rank + 1) * ROWS, :]
            tiles.append(tile.astype(jnp.float32))
        for i, tile in enumerate(swap_quads(tiles)):
            lhs_ref[i * ROWS : (i + 1) * ROWS, group * LANES : (group + 1) * LANES] = tile.astype(
                lhs_ref.dtype
            )

    groups = width // LANES

    def chunk(n, carry):
        copy(n).wait()
        part = jnp.dot(lhs_ref[...], held_ref[n], preferred_element_type=jnp.float32)
        for group in range(groups):
            lanes = slice(group * LANES, (group + 1) * LANES)
            tiles = [part[i * ROWS : (i + 1) * ROWS, lanes] for i in range(QUADS)]
            for m, tile in enumerate(swap_quads(tiles)):
                out_ref[spot_ref[(n * groups + group) * QUADS + m]] = tile
        return carry

    lax.fori_loop(0, chunks, chunk, 0)


def weights_call(order, stations, weight):
    count = order.shape[0]
    depth, observers = weight.shape
    width = 512
    return pl.pallas_call(
        weights_kernel,
        name="observers",
        out_shape=jax.ShapeDtypeStruct((count, ROWS, LANES), jnp.float32),
        in_specs=[IN_SMEM, IN_VMEM, ANY],
        out_specs=IN_VMEM,
        scratch_shapes=[
            pltpu.VMEM((NT, depth), jnp.bfloat16),
            pltpu.VMEM((observers // width, depth, width), jnp.bfloat16),
            pltpu.SMEM((count,), jnp.int32),
            pltpu.SemaphoreType.DMA((observers // width,)),
        ],
        compiler_params=limits(14),
        cost_estimate=cost(2 * NT * depth * observers, 2 * depth * observers),
    )(order, stations, in_hbm(weight))


def retard_kernel(parts_ref, matrix_ref, out_ref, times_ref, late_ref):
    def add(i, total):
        for j in range(8):
            total = total + parts_ref[i * 8 + j]
        return total

    total = lax.fori_loop(
        0, parts_ref.shape[0] // 8, add, jnp.zeros(parts_ref.shape[1:], jnp.float32)
    )
    for i in range(QUADS):
        turned = total if i == 0 else pltpu.roll(total, LANES - i * BP, 1)
        times_ref[pl.ds(i, ROWS, stride=QUADS), :] = turned
    late_ref[...] = jnp.dot(
        matrix_ref[...],
        times_ref[...],
        precision=lax.Precision.HIGHEST,
        preferred_element_type=jnp.float32,
    )
    lane = lax.broadcasted_iota(jnp.int32, (ROWS, LANES), 1)
    out = late_ref[pl.ds(0, ROWS, stride=QUADS), :]
    for i in range(1, QUADS):
        tile = pltpu.roll(late_ref[pl.ds(i, ROWS, stride=QUADS), :], i * BP, 1)
        out = jnp.where(lane >= i * BP, tile, out)
    out_ref[...] = out


def retard_call(parts, matrix):
    return pl.pallas_call(
        retard_kernel,
        name="retard",
        out_shape=jax.ShapeDtypeStruct((ROWS, LANES), jnp.float32),
        in_specs=[pl.BlockSpec(memory_space=pltpu.VMEM)] * 2,
        out_specs=pl.BlockSpec(memory_space=pltpu.VMEM),
        scratch_shapes=[pltpu.VMEM((NT, LANES), jnp.float32)] * 2,
        compiler_params=limits(4),
        cost_estimate=cost(2 * parts.size, 4 * parts.size),
    )(parts, matrix)


def exchange(first, last, axis, wrap):
    count = lax.axis_size(axis)
    up = [(i, (i + 1) % count) for i in range(count if wrap else count - 1)]
    down = [(j, i) for i, j in up]
    return lax.ppermute(last, axis, up), lax.ppermute(first, axis, down)


def neighbours(packed):
    az_first, az_last, rad_first, rad_last = packed
    rad = exchange(rad_first, rad_last, "radius", False)
    az = exchange(az_first, az_last, "azimuth", True)
    return az, rad


def per_device(
    flow_state,
    base_state,
    mean_flow,
    panel_history,
    panel_line,
    panel_start,
    panel_count,
    panel_owner,
    source_weight,
    retarded_time,
    observer_block,
):
    az0, rad0 = neighbours(pack_call(flow_state, FIRST_AZ, FIRST_RAD))
    slots = (panel_owner, panel_count.T)
    history, local, coef = panels_call(
        *slots, panel_line, mean_flow, flow_state, base_state, panel_history[0, 0]
    )
    outgoing = fresh_call(*slots, panel_line, panel_start, coef, local, az0, rad0, history)
    stations = lax.all_to_all(outgoing, "azimuth", split_axis=0, concat_axis=0, tiled=True)
    later, _ = lax.optimization_barrier((flow_state, outgoing))
    packed = pack_call(later, LATER_AZ, LATER_RAD)
    az1, rad1 = neighbours(packed)
    sends = weights_call(observer_block, stations, source_weight[0])
    parts = lax.all_to_all(sends, BOTH, split_axis=0, concat_axis=0, tiled=True)
    next_state = fields_call(flow_state, az0, az1, base_state, rad0, rad1, coef)

    chosen = lax.dynamic_index_in_dim(observer_block, lax.axis_index(BOTH), 0, keepdims=False)
    blocks = lax.broadcasted_iota(jnp.int32, retarded_time.shape, 0)
    matrix = jnp.sum(jnp.where(blocks == chosen, retarded_time, 0.0), axis=0)
    pressure = retard_call(parts, matrix)
    return next_state, pressure.reshape(1, ROWS * LANES)


def solution(mesh):
    placed = (
        P(None, "azimuth", "radius", None),
        P(None, "azimuth", "radius", None),
        P(None, "radius"),
        P("azimuth", "radius", None, None),
        P("azimuth", "radius", None),
        P("azimuth", "radius", None),
        P(),
        P(),
        P("radius", "azimuth", None),
        P(),
        P(),
    )

    return jax.shard_map(
        per_device,
        mesh=mesh,
        in_specs=placed,
        out_specs=(P(None, "azimuth", "radius", None), P(BOTH, None)),
        check_vma=False,
    )
```

time: 884 us -> 90.7 us (0.10)
  waiting for transfers between devices: 646 us -> 13.3 us
  local copies, waits for them, and re-layouts: 141 us -> 0.63 us
  other arithmetic: 56.1 us -> 1.26 us
  Pallas kernels: 0 us -> 34.4 us
  between operations: 16.3 us -> 0.88 us
  blocking collectives: 0 us -> 12.5 us
  starting transfers between devices: 15.1 us -> 27.1 us
    reduce_scatter x1 -> x0, waiting for transfers between devices: 642 us -> none  [per_device(): lax.psum_scatter(ordered, ('azimuth', 'radius'), scatter_dimension=1, til...]
    dot_general x3 -> x0, local copies, waits for them, and re-layouts: 66.7 us -> none  [per_device(): jnp.einsum('stp,spo->to', stations.reshape(total_stations, NT, BP), weigh...]
    gather x49 -> x0, local copies, waits for them, and re-layouts: 34.9 us -> none
    pallas_call x0 -> x7, Pallas kernels: none -> 34.4 us  [the longest x1 15.6 us: fields_call(): pl.pallas_call(fields_kernel, name='fields', out_shape=jax.ShapeDtypeStru...]
    unnamed x4 -> x0, other arithmetic: 24 us -> none
    add x1 -> x0, other arithmetic: 20.9 us -> none  [per_device(): base_state + SECTION_STEP * tendency(flow_state, cycle_ext, band_ext, mea...]
    all_to_all x0 -> x1, blocking collectives: none -> 12.5 us  [per_device(): lax.all_to_all(outgoing, 'azimuth', split_axis=0, concat_axis=0, tiled=True)]
    another operation x2 -> x0, local copies, waits for them, and re-layouts: 12.2 us -> none  [the longest x1 11.2 us: per_device(): weights = source_weight[0].reshape(total_stations, BP, OBS)]
  transfers between devices with their start and end apart: 6 -> 9, of which waited for: 2 -> 3; matrix products, arithmetic and copies ran while one was open for 12% -> 2% of each run, Pallas kernels for 0% -> 25%
where the time goes in v2:
time: 90.7 us; the launch traced here: 90.1 us
  Pallas kernels  34.4 us (38%)
  starting transfers between devices  27.1 us (30%)
  waiting for transfers between devices  13.3 us (15%)
  blocking collectives  12.5 us (14%)
  other arithmetic  1.26 us (1%)
    ppermute x8, starting transfers between devices, exchange(): return (lax.ppermute(last, axis, up), lax.ppermute(first, axis, down))  19.9 us
    pallas_call x1, Pallas kernels, fields_call(): pl.pallas_call(fields_kernel, name='fields', out_shape=jax.ShapeDtypeStru...  15.6 us
    ppermute x8, waiting for transfers between devices, exchange(): return (lax.ppermute(last, axis, up), lax.ppermute(first, axis, down))  13.3 us
    all_to_all x1, blocking collectives, per_device(): lax.all_to_all(outgoing, 'azimuth', split_axis=0, concat_axis=0, tiled=True)  12.5 us
    all_to_all x1, starting transfers between devices, per_device(): parts = lax.all_to_all(sends, BOTH, split_axis=0, concat_axis=0, tiled=True)  7.2 us
    pallas_call x1, Pallas kernels, weights_call(): pl.pallas_call(weights_kernel, name='observers', out_shape=jax.ShapeDtype...  6.49 us
    pallas_call x1, Pallas kernels, panels_call(): pl.pallas_call(panels_kernel, name='panels', out_shape=(jax.ShapeDtypeStr...  5.25 us
    pallas_call x2, Pallas kernels, pack_call(): pl.pallas_call(functools.partial(pack_kernel, az=az, rad=rad), out_shape=...  3.1 us
  transfers between devices with their start and end apart: 9, of which 3 were waited for; matrix products, arithmetic and copies ran while one was open for 2% of the time, Pallas kernels for 25%

profile of v2, /device:TPU:0, one launch (start us, length us, event | category | flops | bytes accessed | tf_op | source)
XLA Modules:
  0.0 90.1 jit_solution(17470394779426669321)
XLA Ops:
  0.7 1.5 %shard_map.122 = (f32[2,2,32,384]{3,2,1,0:T(8,128)S(1)}, f32[2,2,32,384]{3,2,1,0:T(8,128)S(1)}, f32[16,4,384]{2,1,0:T(4,128)S(1)}, f32[16,4,384]{2,1,0:T(4,128)S(1)}) custom-call(f32[5,16,32,384]{3,2,1,0:T(8,128)} %flow_ref.6), custom_call_target="tpu_custom_call" | custom-call | bytes 786432 | tf_op jit(solution)/shard_map/pallas_call | solution.py:515
  2.1 0.1 collective-permute-start
  2.2 6.3 %collective-permute-start.1 = (f32[2,2,32,384]{3,2,1,0:T(8,128)S(1)}, f32[2,2,32,384]{3,2,1,0:T(8,128)S(1)}, u32[]{:S(2)}, u32[]{:S(2)}) collective-permute-start(f32[2,2,32,384]{3,2,1,0:T(8,128)S(1)} %get-tuple-element.15), channel_id=1, source_target_pairs={{8,0},{16,8},{24,16},{32,24},{40,32},{48,40},{56,48},{64,56},{72,6... | collective-permute-start | bytes 589832 | tf_op jit(solution)/shard_map/ppermute | solution.py:707
  8.5 2.6 %collective-permute-start.2 = (f32[16,4,384]{2,1,0:T(4,128)S(1)}, f32[16,4,384]{2,1,0:T(4,128)S(1)}, u32[]{:S(2)}, u32[]{:S(2)}) collective-permute-start(f32[16,4,384]{2,1,0:T(4,128)S(1)} %get-tuple-element.18), channel_id=1, source_target_pairs={{0,1},{1,2},{2,3},{3,4},{4,5},{5,6},{6,7},{8,9},{9,10},{10,11},{11... | collective-permute-start | bytes 294920 | tf_op jit(solution)/shard_map/ppermute | solution.py:707
  11.2 1.3 %collective-permute-start.3 = (f32[16,4,384]{2,1,0:T(4,128)S(1)}, f32[16,4,384]{2,1,0:T(4,128)S(1)}, u32[]{:S(2)}, u32[]{:S(2)}) collective-permute-start(f32[16,4,384]{2,1,0:T(4,128)S(1)} %get-tuple-element.19), channel_id=1, source_target_pairs={{1,0},{2,1},{3,2},{4,3},{5,4},{6,5},{7,6},{9,8},{10,9},{11,10},{12... | collective-permute-start | bytes 294920 | tf_op jit(solution)/shard_map/ppermute | solution.py:707
  12.5 5.2 %panels.1 = (bf16[16,32,128]{2,1,0:T(8,128)(2,1)S(1)}, f32[16,8,128]{2,1,0:T(8,128)S(1)}, f32[11,32,128]{2,1,0:T(8,128)S(1)}) custom-call(s32[16,8,16]{2,1,0:T(8,128)S(1)} %copy-done, s32[8,16]{1,0:T(8,128)S(1)} %bitcast.6, s32[1,1,16]{2,1,0:T(1,128)S(1)} %copy-done.3, f32[2,32]{1,0:T(2,128)S(1)} %copy-done.4, f32[5,16,32,384]{3,2,1,0:T(8,128)} %flow_ref.6, ...), custom_call_target="tpu_custom_call" | custom-call | bytes 3932160 | tf_op jit(solution)/shard_map/panels/pallas_call | solution.py:532
  17.8 0.1 collective-permute-done.3.hi_ref.hi0_ref
  17.9 2.9 %fresh.1 = bf16[16,32,128]{2,1,0:T(8,128)(2,1)S(1)} custom-call(s32[16,8,16]{2,1,0:T(8,128)S(1)} %copy-done, s32[8,16]{1,0:T(8,128)S(1)} %bitcast.7, s32[1,1,16]{2,1,0:T(1,128)S(1)} %copy-done.3, s32[1,1,16]{2,1,0:T(1,128)S(1)} %copy-done.5, f32[11,32,128]{2,1,0:T(8,128)S(1)} %get-tuple-element.16.coef_ref, f32[16,8,128]{2,1,0:T(8,128)S(1)} %get-tuple-element.17.rows_ref, ...), custom_call_target="tpu_custom_call" | custom-call | bytes 786432 | tf_op jit(solution)/shard_map/fresh/pallas_call | solution.py:557
  20.8 12.5 %all_to_all.10.stations_ref = bf16[16,32,128]{2,1,0:T(8,128)(2,1)S(1)} all-to-all(bf16[16,32,128]{2,1,0:T(8,128)(2,1)S(1)} %fresh.1), channel_id=1, replica_groups=mesh['azimuth'=16,'radius'=8] {'azimuth'}, dimensions={0} | all-to-all | bytes 262144 | tf_op jit(solution)/shard_map/all_to_all | solution.py:736
  33.3 6.5 %observers.1 = f32[128,16,128]{2,1,0:T(8,128)} custom-call(s32[128]{0:T(128)S(1)} %copy-done.6, bf16[16,32,128]{2,1,0:T(8,128)(2,1)S(1)} %all_to_all.10.stations_ref, bf16[1024,4096]{1,0:T(8,128)(2,1)} %bitcast.8), custom_call_target="tpu_custom_call" | custom-call | flops 536870912 | bytes 8388608 | tf_op jit(solution)/shard_map/observers/pallas_call | solution.py:647
  39.8 7.2 %all-to-all-start.1 = ((f32[128,16,128]{2,1,0:T(8,128)}), f32[128,16,128]{2,1,0:T(8,128)S(1)}, u32[]{:S(2)}, u32[]{:S(2)}) async-start(f32[128,16,128]{2,1,0:T(8,128)} %observers.1), calls=%async_computation.1 | async-start | bytes 2097152 | tf_op jit(solution)/shard_map/all_to_all | solution.py:741
  47.0 0.0 copy-start.7
  47.0 0.6 dynamic_slice.4
  47.6 1.6 %shard_map.123 = (f32[3,2,32,384]{3,2,1,0:T(8,128)S(1)}, f32[3,2,32,384]{3,2,1,0:T(8,128)S(1)}, f32[16,6,384]{2,1,0:T(8,128)S(1)}, f32[16,6,384]{2,1,0:T(8,128)S(1)}) custom-call(f32[5,16,32,384]{3,2,1,0:T(8,128)} %flow_ref.6), custom_call_target="tpu_custom_call" | custom-call | bytes 1179648 | tf_op jit(solution)/shard_map/pallas_call | solution.py:515
  49.3 0.1 collective-permute-start.4
  49.3 5.3 %collective-permute-start.5 = (f32[3,2,32,384]{3,2,1,0:T(8,128)S(1)}, f32[3,2,32,384]{3,2,1,0:T(8,128)S(1)}, u32[]{:S(2)}, u32[]{:S(2)}) collective-permute-start(f32[3,2,32,384]{3,2,1,0:T(8,128)S(1)} %get-tuple-element.23), channel_id=1, source_target_pairs={{8,0},{16,8},{24,16},{32,24},{40,32},{48,40},{56,48},{64,56},{72,6... | collective-permute-start | bytes 884744 | tf_op jit(solution)/shard_map/ppermute | solution.py:707
  54.7 0.6 iota_compare_fusion
  55.4 2.9 %collective-permute-start.6 = (f32[16,6,384]{2,1,0:T(8,128)S(1)}, f32[16,6,384]{2,1,0:T(8,128)S(1)}, u32[]{:S(2)}, u32[]{:S(2)}) collective-permute-start(f32[16,6,384]{2,1,0:T(8,128)S(1)} %get-tuple-element.24), channel_id=1, source_target_pairs={{0,1},{1,2},{2,3},{3,4},{4,5},{5,6},{6,7},{8,9},{9,10},{10,11},{11... | collective-permute-start | bytes 442376 | tf_op jit(solution)/shard_map/ppermute | solution.py:707
  58.2 1.3 %collective-permute-start.7 = (f32[16,6,384]{2,1,0:T(8,128)S(1)}, f32[16,6,384]{2,1,0:T(8,128)S(1)}, u32[]{:S(2)}, u32[]{:S(2)}) collective-permute-start(f32[16,6,384]{2,1,0:T(8,128)S(1)} %get-tuple-element.25), channel_id=1, source_target_pairs={{1,0},{2,1},{3,2},{4,3},{5,4},{6,5},{7,6},{9,8},{10,9},{11,10},{12... | collective-permute-start | bytes 442376 | tf_op jit(solution)/shard_map/ppermute | solution.py:707
  59.5 0.6 select_reduce_fusion.matrix_ref
  60.2 9.6 %collective-permute-done.6.lo1_ref = f32[16,6,384]{2,1,0:T(8,128)S(1)} collective-permute-done((f32[16,6,384]{2,1,0:T(8,128)S(1)}, f32[16,6,384]{2,1,0:T(8,128)S(1)}, u32[]{:S(2)}, u32[]{:S(2)}) %collective-permute-start.6) | collective-permute-done | bytes 147488 | tf_op jit(solution)/shard_map/ppermute | solution.py:707
  69.7 3.7 %collective-permute-done.4.before1_ref = f32[3,2,32,384]{3,2,1,0:T(8,128)S(1)} collective-permute-done((f32[3,2,32,384]{3,2,1,0:T(8,128)S(1)}, f32[3,2,32,384]{3,2,1,0:T(8,128)S(1)}, u32[]{:S(2)}, u32[]{:S(2)}) %collective-permute-start.4) | collective-permute-done | bytes 294944 | tf_op jit(solution)/shard_map/ppermute | solution.py:707
  73.4 15.6 %fields.1 = f32[5,16,32,384]{3,2,1,0:T(8,128)} custom-call(f32[5,16,32,384]{3,2,1,0:T(8,128)} %flow_ref.6, f32[2,2,32,384]{3,2,1,0:T(8,128)S(1)} %collective-permute-done.before_ref.before0_ref, f32[2,2,32,384]{3,2,1,0:T(8,128)S(1)} %collective-permute-done.1.after_ref.after0_ref, f32[3,2,32,384]{3,2,1,0:T(8,128)S(1)} %collective-permute-done.4.before1_ref, ...), custom_call_target="tpu_custom_call" | custom-call | flops 49152000 | bytes 11796480 | tf_op jit(solution)/shard_map/fields/pallas_call | solution.py:578
  89.0 1.1 %retard.1 = f32[16,128]{1,0:T(8,128)} custom-call(f32[128,16,128]{2,1,0:T(8,128)S(1)} %all-to-all-done.1.parts_ref, f32[64,64]{1,0:T(8,128)S(1)} %select_reduce_fusion.matrix_ref), custom_call_target="tpu_custom_call" | custom-call | flops 524288 | bytes 1048576 | tf_op jit(solution)/shard_map/retard/pallas_call | solution.py:691
  (21 shorter events, 0.1 us)
Async XLA Ops:
  0.6 11.8 %copy-start = (s32[16,8,16]{2,1,0:T(8,128)S(1)}, s32[16,8,16]{2,1,0:T(8,128)}, u32[]{:S(2)}) copy-start(s32[16,8,16]{2,1,0:T(8,128)} %owner_ref.3) | copy-start | bytes 24580
  0.6 11.8 %copy-start.3 = (s32[1,1,16]{2,1,0:T(1,128)S(1)}, s32[1,1,16]{2,1,0:T(1,128)}, u32[]{:S(2)}) copy-start(s32[1,1,16]{2,1,0:T(1,128)} %line_ref.3) | copy-start | bytes 196
  0.7 11.8 %copy-start.2 = (s32[16,8]{0,1:T(8,128)S(1)}, s32[16,8]{0,1:T(8,128)}, u32[]{:S(2)}) copy-start(s32[16,8]{0,1:T(8,128)} %param.17) | copy-start | bytes 1540
  0.7 11.8 %copy-start.1 = (bf16[1,1,16,2016]{3,2,1,0:T(8,128)(2,1)S(1)}, bf16[1,1,16,2016]{3,2,1,0:T(8,128)(2,1)}, u32[]{:S(2)}) copy-start(bf16[1,1,16,2016]{3,2,1,0:T(8,128)(2,1)} %param.14) | copy-start | bytes 193540
  0.7 11.8 %copy-start.4 = (f32[2,32]{1,0:T(2,128)S(1)}, f32[2,32]{1,0:T(2,128)}, u32[]{:S(2)}) copy-start(f32[2,32]{1,0:T(2,128)} %mean_ref.1) | copy-start | bytes 772
  2.1 15.7 %collective-permute-start = (f32[2,2,32,384]{3,2,1,0:T(8,128)S(1)}, f32[2,2,32,384]{3,2,1,0:T(8,128)S(1)}, u32[]{:S(2)}, u32[]{:S(2)}) collective-permute-start(f32[2,2,32,384]{3,2,1,0:T(8,128)S(1)} %get-tuple-element.14), channel_id=1, source_target_pairs={{0,8},{8,16},{16,24},{24,32},{32,40},{40,48},{48,56},{56,64},{64,7... | collective-permute-start | bytes 589832 | tf_op jit(solution)/shard_map/ppermute | solution.py:707
  2.2 15.6 %collective-permute-start.1 = (f32[2,2,32,384]{3,2,1,0:T(8,128)S(1)}, f32[2,2,32,384]{3,2,1,0:T(8,128)S(1)}, u32[]{:S(2)}, u32[]{:S(2)}) collective-permute-start(f32[2,2,32,384]{3,2,1,0:T(8,128)S(1)} %get-tuple-element.15), channel_id=1, source_target_pairs={{8,0},{16,8},{24,16},{32,24},{40,32},{48,40},{56,48},{64,56},{72,6... | collective-permute-start | bytes 589832 | tf_op jit(solution)/shard_map/ppermute | solution.py:707
  8.5 9.3 %collective-permute-start.2 = (f32[16,4,384]{2,1,0:T(4,128)S(1)}, f32[16,4,384]{2,1,0:T(4,128)S(1)}, u32[]{:S(2)}, u32[]{:S(2)}) collective-permute-start(f32[16,4,384]{2,1,0:T(4,128)S(1)} %get-tuple-element.18), channel_id=1, source_target_pairs={{0,1},{1,2},{2,3},{3,4},{4,5},{5,6},{6,7},{8,9},{9,10},{10,11},{11... | collective-permute-start | bytes 294920 | tf_op jit(solution)/shard_map/ppermute | solution.py:707
  11.2 6.7 %collective-permute-start.3 = (f32[16,4,384]{2,1,0:T(4,128)S(1)}, f32[16,4,384]{2,1,0:T(4,128)S(1)}, u32[]{:S(2)}, u32[]{:S(2)}) collective-permute-start(f32[16,4,384]{2,1,0:T(4,128)S(1)} %get-tuple-element.19), channel_id=1, source_target_pairs={{1,0},{2,1},{3,2},{4,3},{5,4},{6,5},{7,6},{9,8},{10,9},{11,10},{12... | collective-permute-start | bytes 294920 | tf_op jit(solution)/shard_map/ppermute | solution.py:707
  12.5 5.4 %copy-start.5 = (s32[1,1,16]{2,1,0:T(1,128)S(1)}, s32[1,1,16]{2,1,0:T(1,128)}, u32[]{:S(2)}) copy-start(s32[1,1,16]{2,1,0:T(1,128)} %start_ref.1) | copy-start | bytes 196
  12.5 20.8 %copy-start.6 = (s32[128]{0:T(128)S(1)}, s32[128]{0:T(128)}, u32[]{:S(2)}) copy-start(s32[128]{0:T(128)} %order_ref.1) | copy-start | bytes 1540
  39.8 49.2 %all-to-all-start.1 = ((f32[128,16,128]{2,1,0:T(8,128)}), f32[128,16,128]{2,1,0:T(8,128)S(1)}, u32[]{:S(2)}, u32[]{:S(2)}) async-start(f32[128,16,128]{2,1,0:T(8,128)} %observers.1), calls=%async_computation.1 | async-start | bytes 2097152 | tf_op jit(solution)/shard_map/all_to_all | solution.py:741
  47.0 12.5 %copy-start.7 = (f32[128,64,64]{0,2,1:T(8,128)S(1)}, f32[128,64,64]{0,2,1:T(8,128)}, u32[]{:S(2)}) copy-start(f32[128,64,64]{0,2,1:T(8,128)} %param.20) | copy-start | bytes 6291460
  49.3 24.1 %collective-permute-start.4 = (f32[3,2,32,384]{3,2,1,0:T(8,128)S(1)}, f32[3,2,32,384]{3,2,1,0:T(8,128)S(1)}, u32[]{:S(2)}, u32[]{:S(2)}) collective-permute-start(f32[3,2,32,384]{3,2,1,0:T(8,128)S(1)} %get-tuple-element.22), channel_id=1, source_target_pairs={{0,8},{8,16},{16,24},{24,32},{32,40},{40,48},{48,56},{56,64},{64,7... | collective-permute-start | bytes 884744 | tf_op jit(solution)/shard_map/ppermute | solution.py:707
  49.3 24.1 %collective-permute-start.5 = (f32[3,2,32,384]{3,2,1,0:T(8,128)S(1)}, f32[3,2,32,384]{3,2,1,0:T(8,128)S(1)}, u32[]{:S(2)}, u32[]{:S(2)}) collective-permute-start(f32[3,2,32,384]{3,2,1,0:T(8,128)S(1)} %get-tuple-element.23), channel_id=1, source_target_pairs={{8,0},{16,8},{24,16},{32,24},{40,32},{48,40},{56,48},{64,56},{72,6... | collective-permute-start | bytes 884744 | tf_op jit(solution)/shard_map/ppermute | solution.py:707
  55.4 14.4 %collective-permute-start.6 = (f32[16,6,384]{2,1,0:T(8,128)S(1)}, f32[16,6,384]{2,1,0:T(8,128)S(1)}, u32[]{:S(2)}, u32[]{:S(2)}) collective-permute-start(f32[16,6,384]{2,1,0:T(8,128)S(1)} %get-tuple-element.24), channel_id=1, source_target_pairs={{0,1},{1,2},{2,3},{3,4},{4,5},{5,6},{6,7},{8,9},{9,10},{10,11},{11... | collective-permute-start | bytes 442376 | tf_op jit(solution)/shard_map/ppermute | solution.py:707
  58.2 11.5 %collective-permute-start.7 = (f32[16,6,384]{2,1,0:T(8,128)S(1)}, f32[16,6,384]{2,1,0:T(8,128)S(1)}, u32[]{:S(2)}, u32[]{:S(2)}) collective-permute-start(f32[16,6,384]{2,1,0:T(8,128)S(1)} %get-tuple-element.25), channel_id=1, source_target_pairs={{1,0},{2,1},{3,2},{4,3},{5,4},{6,5},{7,6},{9,8},{10,9},{11,10},{12... | collective-permute-start | bytes 442376 | tf_op jit(solution)/shard_map/ppermute | solution.py:707

commit v3 on v2

--- a/solution.py
+++ b/solution.py
@@ -15,15 +15,14 @@
 LANES = 128
 ROWS = NT * BP // LANES
 QUADS = LANES // BP
+WIDTH = 512
 
 SECTION_STEP = 0.3
 VISCOSITY = 0.05
 BOTH = ("azimuth", "radius")
 
 NVAR = 5
-FIRST_AZ = (1, 4)
 FIRST_RAD = (2, 4)
-LATER_AZ = (0, 2, 3)
 LATER_RAD = (0, 1, 3)
 
 
@@ -47,57 +46,25 @@
     )
 
 
-ORDER = FIRST_AZ + LATER_AZ
 EDGE = 8
 CHUNK = 4
 
 
-def plane_copies(flow_ref, before_refs, after_refs, ext_ref, sems):
+def plane_copies(flow_ref, before_ref, after_ref, ext_ref, sems):
     planes, rows, length = flow_ref.shape[1:]
+    sources = [(before_ref, 0, 0, 2)]
+    for first in range(0, planes, CHUNK):
+        sources.append((flow_ref, first, first + 2, CHUNK))
+    sources.append((after_ref, 0, planes + 2, 2))
     stages = []
-
-    def put(src, place, spots, t, stage):
-        dst = ext_ref.at[place, spots, t, pl.ds(EDGE, rows)]
-        stages[-1].append(pltpu.make_async_copy(src, dst, sems.at[stage, place, t]))
-
-    def layers(refs, spot, stage):
-        place = 0
-        for ref in refs:
-            for s in range(ref.shape[0]):
-                for t in range(length // LANES):
-                    src = ref.at[s, :, :, pl.ds(t * LANES, LANES)]
-                    put(src, place, pl.ds(spot, 2), t, stage)
-                place += 1
-
-    stages.append([])
-    layers(before_refs, 0, 0)
-    for c in range(planes // CHUNK):
+    for stage, (ref, first, spot, count) in enumerate(sources):
         stages.append([])
-        for place, var in enumerate(ORDER):
+        for var in range(NVAR):
             for t in range(length // LANES):
-                at = pl.ds(c * CHUNK, CHUNK)
-                src = flow_ref.at[var, at, :, pl.ds(t * LANES, LANES)]
-                put(src, place, pl.ds(c * CHUNK + 2, CHUNK), t, c + 1)
-    stages.append([])
-    layers(after_refs, planes + 2, planes // CHUNK + 1)
+                src = ref.at[var, pl.ds(first, count), :, pl.ds(t * LANES, LANES)]
+                dst = ext_ref.at[var, pl.ds(spot, count), t, pl.ds(EDGE, rows)]
+                stages[-1].append(pltpu.make_async_copy(src, dst, sems.at[stage, var, t]))
     return stages
-
-
-def feed_planes(a, stages):
-    @pl.when(a == 0)
-    def _():
-        for stage in stages:
-            for c in stage:
-                c.start()
-        for c in stages[0] + stages[1]:
-            c.wait()
-
-    for i, stage in enumerate(stages[2:]):
-
-        @pl.when(a == (i + 1) * CHUNK - 2)
-        def _():
-            for c in stage:
-                c.wait()
 
 
 def axial_shifts(tiles):
@@ -159,21 +126,25 @@
     return totals
 
 
-def pack_kernel(flow_ref, az_first_ref, az_last_ref, rad_first_ref, rad_last_ref, edge_ref, sems, *, az, rad):
+def pack_kernel(flow_ref, *refs, rad, with_az):
+    *outs, edge_ref, sems = refs
+    rad_first_ref, rad_last_ref = outs[-2:]
     planes, rows = flow_ref.shape[1:3]
     direct, edges = [], []
     for s, var in enumerate(rad):
-        for side, start in enumerate((0, rows - 8)):
+        for side, start in enumerate((0, rows - EDGE)):
             edges.append(
                 pltpu.make_async_copy(
-                    flow_ref.at[var, :, pl.ds(start, 8)], edge_ref.at[side, s], sems.at[1, side, s]
+                    flow_ref.at[var, :, pl.ds(start, EDGE)],
+                    edge_ref.at[side, s],
+                    sems.at[side, s],
                 )
             )
-    for s, var in enumerate(az):
-        for side, (ref, start) in enumerate(((az_first_ref, 0), (az_last_ref, planes - 2))):
+    if with_az:
+        for side, (ref, start) in enumerate(zip(outs, (0, planes - 2))):
             direct.append(
                 pltpu.make_async_copy(
-                    flow_ref.at[var, pl.ds(start, 2)], ref.at[s], sems.at[0, side, s]
+                    flow_ref.at[:, pl.ds(start, 2)], ref, sems.at[side, len(rad)]
                 )
             )
     for c in edges + direct:
@@ -183,29 +154,9 @@
     for a in range(planes):
         for s in range(len(rad)):
             rad_first_ref[a, 2 * s : 2 * s + 2, :] = edge_ref[0, s, a, 0:2, :]
-            rad_last_ref[a, 2 * s : 2 * s + 2, :] = edge_ref[1, s, a, 6:8, :]
+            rad_last_ref[a, 2 * s : 2 * s + 2, :] = edge_ref[1, s, a, EDGE - 2 : EDGE, :]
     for c in direct:
         c.wait()
-
-
-def slots_of(count_ref):
-    cycle, band = lax.axis_index("azimuth"), lax.axis_index("radius")
-    return cycle, band, count_ref[band, cycle]
-
-
-def for_live_slots(owner_ref, count_ref, rank_ref, visit):
-    cycle, band, count = slots_of(count_ref)
-    for q in range(rank_ref.shape[0]):
-        rank_ref[q] = 0
-
-    def one(k, carry):
-        owner = owner_ref[cycle, band, k]
-        rank = rank_ref[owner]
-        rank_ref[owner] = rank + 1
-        visit(k, owner, rank)
-        return carry
-
-    lax.fori_loop(0, count, one, 0)
 
 
 def fill_coefficients(coef_ref, mean_ref, planes):
@@ -244,10 +195,12 @@
     out_ref,
     rows_ref,
     coef_ref,
+    slots_ref,
     store_ref,
     wide_ref,
     block_ref,
     rank_ref,
+    own_ref,
     sems,
 ):
     planes, tiles, band = store_ref.shape[1:4]
@@ -259,8 +212,13 @@
         for s, (ref, var) in enumerate(sources)
         for t in range(tiles)
     ]
+    cycle, radius = lax.axis_index("azimuth"), lax.axis_index("radius")
+    owners = pltpu.make_async_copy(owner_ref.at[cycle], own_ref, sems.at[len(sources), 0])
+    owners.start()
     for c in copies:
         c.start()
+    count = count_ref[radius, cycle]
+    slots_ref[2 * KMAX] = count
     fill_coefficients(coef_ref, mean_ref, planes)
     wide_ref[ROWS - 1] = jnp.zeros_like(wide_ref[ROWS - 1])
     for r in range(ROWS):
@@ -269,13 +227,23 @@
         wide_ref[r, :, 0:width] = chunk.astype(jnp.float32)
     out_ref[...] = jnp.zeros_like(out_ref)
 
-    def place(k, owner, rank):
+    for q in range(rank_ref.shape[0]):
+        rank_ref[q] = 0
+    owners.wait()
+
+    def place(k, carry):
+        owner = own_ref[radius, k]
+        rank = rank_ref[owner]
+        rank_ref[owner] = rank + 1
+        slots_ref[k] = owner
+        slots_ref[KMAX + k] = rank
         for r in range(ROWS):
             block_ref[r : r + 1, :] = wide_ref[r, pl.ds(k, 1), :]
         at = pl.ds(pl.multiple_of(rank * ROWS, ROWS), ROWS)
         out_ref[owner, at, :] = block_ref[...].astype(out_ref.dtype)
-
-    for_live_slots(owner_ref, count_ref, rank_ref, place)
+        return carry
+
+    lax.fori_loop(0, count, place, 0)
     for c in copies:
         c.wait()
 
@@ -336,12 +304,11 @@
             rows_ref[k, t : t + 1, :] = total[t]
         return carry
 
-    lax.fori_loop(0, slots_of(count_ref)[2], local, 0)
+    lax.fori_loop(0, count, local, 0)
 
 
 def fresh_kernel(
-    owner_ref,
-    count_ref,
+    slots_ref,
     line_ref,
     start_ref,
     coef_ref,
@@ -354,15 +321,19 @@
     out_ref,
     ring_ref,
     sum_ref,
-    rank_ref,
+    sems,
 ):
     tiles, band = ring_ref.shape[1:3]
     planes = lo_ref.shape[0]
-    for s in range(2):
+    copies = []
+    for s, var in enumerate((1, 4)):
         for side, ref in enumerate((before_ref, after_ref)):
-            for j in range(2):
-                for t in range(tiles):
-                    ring_ref[4 * s + 2 * side + j, t] = ref[s, j, :, t * LANES : (t + 1) * LANES]
+            for t in range(tiles):
+                src = ref.at[var, :, :, pl.ds(t * LANES, LANES)]
+                dst = ring_ref.at[pl.ds(4 * s + 2 * side, 2), t]
+                copies.append(pltpu.make_async_copy(src, dst, sems.at[s, side, t]))
+    for c in copies:
+        c.start()
     out_ref[...] = held_ref[...]
     lane = lax.broadcasted_iota(jnp.int32, (ROWS, LANES), 1)
     row_of = lax.broadcasted_iota(jnp.int32, (ROWS, LANES), 0)
@@ -379,7 +350,8 @@
             jnp.where(last, far_after, 0.0),
         )
 
-    def put(k, owner, rank):
+    def put(k, carry):
+        owner, rank = slots_ref[k], slots_ref[KMAX + k]
         line, start = line_ref[0, 0, k], start_ref[0, 0, k]
         la, lr = lax.div(line, band), lax.rem(line, band)
         for t in range(tiles):
@@ -422,16 +394,17 @@
         block = out_ref[owner, at, :].astype(jnp.float32)
         place = jnp.logical_and(row_of == ROWS - 1, lane >= LANES - BP)
         out_ref[owner, at, :] = jnp.where(place, window, block).astype(out_ref.dtype)
-
-    for_live_slots(owner_ref, count_ref, rank_ref, put)
+        return carry
+
+    for c in copies:
+        c.wait()
+    lax.fori_loop(0, slots_ref[2 * KMAX], put, 0)
 
 
 def fields_kernel(
     flow_ref,
-    before0_ref,
-    after0_ref,
-    before1_ref,
-    after1_ref,
+    before_ref,
+    after_ref,
     base_ref,
     lo0_ref,
     hi0_ref,
@@ -442,47 +415,65 @@
     ext_ref,
     sems,
 ):
-    a = pl.program_id(0)
-    rows, length = flow_ref.shape[2:]
+    group = pl.program_id(0)
+    planes, rows, length = flow_ref.shape[1:]
     tiles = length // LANES
-    stages = plane_copies(
-        flow_ref, (before0_ref, before1_ref), (after0_ref, after1_ref), ext_ref, sems
-    )
-    feed_planes(a, stages)
-    for var in range(NVAR):
-        if var in FIRST_RAD:
-            lo, hi, s = lo0_ref, hi0_ref, FIRST_RAD.index(var)
-        else:
-            lo, hi, s = lo1_ref, hi1_ref, LATER_RAD.index(var)
-        for t in range(tiles):
-            lanes = slice(t * LANES, (t + 1) * LANES)
-            place = ORDER.index(var)
-            ext_ref[place, a + 2, t, EDGE - 2 : EDGE, :] = lo[a, 2 * s : 2 * s + 2, lanes]
-            ext_ref[place, a + 2, t, EDGE + rows : EDGE + rows + 2, :] = hi[
-                a, 2 * s : 2 * s + 2, lanes
-            ]
-
-    half = 16
-    for start in range(0, rows, half):
-        at = slice(start, start + half)
-
-        def part(var, offset, row_shift):
-            first = EDGE + start + row_shift
-            return [
-                ext_ref[ORDER.index(var), a + 2 + offset, t, first : first + half, :]
-                for t in range(tiles)
-            ]
-
-        def coef(i):
-            return coef_ref[i, at, :]
-
-        def base(var):
-            return [base_ref[var, 0, at, t * LANES : (t + 1) * LANES] for t in range(tiles)]
-
-        totals = plane_update(part, coef, base)
+    stages = plane_copies(flow_ref, before_ref, after_ref, ext_ref, sems)
+
+    def radial_layers(plane, carry):
         for var in range(NVAR):
+            if var in FIRST_RAD:
+                lo, hi, s = lo0_ref, hi0_ref, FIRST_RAD.index(var)
+            else:
+                lo, hi, s = lo1_ref, hi1_ref, LATER_RAD.index(var)
             for t in range(tiles):
-                next_ref[var, 0, at, t * LANES : (t + 1) * LANES] = totals[var][t]
+                at = slice(2 * s, 2 * s + 2), slice(t * LANES, (t + 1) * LANES)
+                ext_ref[var, plane + 2, t, EDGE - 2 : EDGE, :] = lo[(plane, *at)]
+                ext_ref[var, plane + 2, t, EDGE + rows : EDGE + rows + 2, :] = hi[(plane, *at)]
+        return carry
+
+    @pl.when(group == 0)
+    def _():
+        for stage in stages:
+            for c in stage:
+                c.start()
+        lax.fori_loop(0, planes, radial_layers, 0)
+        for c in stages[0] + stages[1]:
+            c.wait()
+
+    def one(inner, carry):
+        a = group * CHUNK + inner
+        for i, stage in enumerate(stages[2:]):
+
+            @pl.when(a == (i + 1) * CHUNK - 2)
+            def _():
+                for c in stage:
+                    c.wait()
+
+        half = 8
+        for start in range(0, rows, half):
+            at = slice(start, start + half)
+
+            def part(var, offset, row_shift):
+                first = EDGE + start + row_shift
+                return [
+                    ext_ref[var, a + 2 + offset, t, first : first + half, :] for t in range(tiles)
+                ]
+
+            held = [coef_ref[i, at, :] for i in range(coef_ref.shape[0])]
+
+            def base(var):
+                return [
+                    base_ref[var, inner, at, t * LANES : (t + 1) * LANES] for t in range(tiles)
+                ]
+
+            totals = plane_update(part, held.__getitem__, base)
+            for var in range(NVAR):
+                for t in range(tiles):
+                    next_ref[var, inner, at, t * LANES : (t + 1) * LANES] = totals[var][t]
+        return carry
+
+    lax.fori_loop(0, CHUNK, one, 0)
 
 
 ANY = pl.BlockSpec(memory_space=pltpu.HBM)
@@ -508,21 +499,22 @@
     return pl.BlockSpec(shape, lambda *_: (0,) * len(shape))
 
 
-def pack_call(flow, az, rad):
-    _, planes, rows, length = flow.shape
-    az_shape = jax.ShapeDtypeStruct((len(az), 2, rows, length), jnp.float32)
+def pack_call(flow, rad, with_az):
+    nvar, planes, rows, length = flow.shape
+    az_shape = jax.ShapeDtypeStruct((nvar, 2, rows, length), jnp.float32)
     rad_shape = jax.ShapeDtypeStruct((planes, 2 * len(rad), length), jnp.float32)
+    shapes = (az_shape,) * (2 * with_az) + (rad_shape,) * 2
     return pl.pallas_call(
-        functools.partial(pack_kernel, az=az, rad=rad),
-        out_shape=(az_shape, az_shape, rad_shape, rad_shape),
+        functools.partial(pack_kernel, rad=rad, with_az=with_az),
+        out_shape=shapes,
         in_specs=[ANY],
-        out_specs=(IN_VMEM,) * 4,
+        out_specs=(IN_VMEM,) * len(shapes),
         scratch_shapes=[
-            pltpu.VMEM((2, len(rad), planes, 8, length), jnp.float32),
-            pltpu.SemaphoreType.DMA((2, 2, max(len(az), len(rad)))),
+            pltpu.VMEM((2, len(rad), planes, EDGE, length), jnp.float32),
+            pltpu.SemaphoreType.DMA((2, len(rad) + 1)),
         ],
         compiler_params=limits(8),
-        cost_estimate=cost(0, 8 * len(az) * 4 * rows * length),
+        cost_estimate=cost(0, 20 * MIB),
     )(in_hbm(flow))
 
 
@@ -536,52 +528,54 @@
             jax.ShapeDtypeStruct((owners, CAP * ROWS, LANES), jnp.bfloat16),
             jax.ShapeDtypeStruct((KMAX, 8, LANES), jnp.float32),
             jax.ShapeDtypeStruct((11, rows, LANES), jnp.float32),
+            jax.ShapeDtypeStruct((LANES,), jnp.int32),
         ),
-        in_specs=[IN_SMEM] * 3 + [IN_VMEM, ANY, ANY, IN_VMEM],
-        out_specs=(IN_VMEM,) * 3,
+        in_specs=[ANY, IN_SMEM, IN_SMEM, IN_VMEM, ANY, ANY, IN_VMEM],
+        out_specs=(IN_VMEM,) * 3 + (IN_SMEM,),
         scratch_shapes=[
             pltpu.VMEM((5, planes, tiles, rows, LANES), jnp.float32),
             pltpu.VMEM((ROWS, KMAX, LANES), jnp.float32),
             pltpu.VMEM((ROWS, LANES), jnp.float32),
             pltpu.SMEM((owners,), jnp.int32),
-            pltpu.SemaphoreType.DMA((5, tiles)),
+            pltpu.SMEM(owner.shape[1:], jnp.int32),
+            pltpu.SemaphoreType.DMA((6, tiles)),
         ],
         compiler_params=limits(8),
         cost_estimate=cost(0, 5 * 4 * planes * rows * length),
-    )(owner, count, line, mean_flow, in_hbm(flow), in_hbm(base), history)
-
-
-def fresh_call(owner, count, line, start, coef, rows, az, rad, held):
+    )(in_hbm(owner), count, line, mean_flow, in_hbm(flow), in_hbm(base), history)
+
+
+def fresh_call(slots, line, start, coef, rows, az, rad, held):
     length = az[0].shape[-1]
     band = az[0].shape[2]
     return pl.pallas_call(
         fresh_kernel,
         name="fresh",
         out_shape=jax.ShapeDtypeStruct(held.shape, held.dtype),
-        in_specs=[IN_SMEM] * 4 + [IN_VMEM] * 7,
+        in_specs=[IN_SMEM] * 3 + [IN_VMEM] * 2 + [pl.BlockSpec(memory_space=pl.ANY)] * 2 + [IN_VMEM] * 3,
         out_specs=IN_VMEM,
         scratch_shapes=[
             pltpu.VMEM((8, length // LANES, band, LANES), jnp.float32),
             pltpu.VMEM((8, LANES), jnp.float32),
-            pltpu.SMEM((held.shape[0],), jnp.int32),
+            pltpu.SemaphoreType.DMA((2, 2, length // LANES)),
         ],
         compiler_params=limits(8),
         cost_estimate=cost(0, 4 * 4 * band * length * 4),
-    )(owner, count, line, start, coef, rows, *az, *rad, held)
-
-
-def fields_call(flow, az0, az1, base, rad0, rad1, coef):
+    )(slots, line, start, coef, rows, *az, *rad, held)
+
+
+def fields_call(flow, az, base, rad0, rad1, coef):
     nvar, planes, rows, length = flow.shape
     cells = planes * rows * length
-    every = (nvar, 1, rows, length)
-    args = (in_hbm(flow), *az0, *az1, in_hbm(base), *rad0, *rad1, coef)
+    every = (nvar, CHUNK, rows, length)
+    args = (in_hbm(flow), *az, in_hbm(base), *rad0, *rad1, coef)
     return pl.pallas_call(
         fields_kernel,
         name="fields",
         out_shape=jax.ShapeDtypeStruct(flow.shape, jnp.float32),
-        grid=(planes,),
+        grid=(planes // CHUNK,),
         in_specs=[
-            *[ANY] + [pl.BlockSpec(memory_space=pl.ANY)] * 4,
+            *[ANY] + [pl.BlockSpec(memory_space=pl.ANY)] * 2,
             pl.BlockSpec(every, lambda a: (0, a, 0, 0)),
             *[whole(x) for x in (*rad0, *rad1, coef)],
         ],
@@ -592,22 +586,26 @@
             ),
             pltpu.SemaphoreType.DMA((planes // CHUNK + 2, nvar, length // LANES)),
         ],
-        compiler_params=limits(14, dimension_semantics=("arbitrary",)),
+        compiler_params=limits(18, dimension_semantics=("arbitrary",)),
         cost_estimate=cost(250 * cells, 15 * 4 * cells),
     )(*args)
 
 
 def weights_kernel(
-    order_ref, stations_ref, weight_ref, out_ref, lhs_ref, held_ref, spot_ref, sems
+    order_ref, stations_ref, weight_ref, out_ref, mask_ref, lhs_ref, held_ref, spot_ref, sems
 ):
     chunks, _, width = held_ref.shape
-
-    def copy(i):
-        at = pl.ds(pl.multiple_of(i * width, width), width)
-        return pltpu.make_async_copy(weight_ref.at[:, at], held_ref.at[i], sems.at[i])
-
-    for i in range(chunks):
-        copy(i).start()
+    copies = [
+        pltpu.make_async_copy(
+            weight_ref.at[:, pl.ds(i * width, width)], held_ref.at[i], sems.at[i]
+        )
+        for i in range(chunks)
+    ]
+    for c in copies:
+        c.start()
+    mine = order_ref[lax.axis_index("azimuth") * lax.axis_size("radius") + lax.axis_index("radius")]
+    block = lax.broadcasted_iota(jnp.int32, mask_ref.shape, 1)
+    mask_ref[...] = jnp.where(block == mine, 1.0, 0.0)
 
     def place(j, carry):
         spot_ref[order_ref[j]] = j
@@ -626,35 +624,33 @@
             )
 
     groups = width // LANES
-
-    def chunk(n, carry):
-        copy(n).wait()
+    for n, c in enumerate(copies):
+        c.wait()
         part = jnp.dot(lhs_ref[...], held_ref[n], preferred_element_type=jnp.float32)
         for group in range(groups):
             lanes = slice(group * LANES, (group + 1) * LANES)
             tiles = [part[i * ROWS : (i + 1) * ROWS, lanes] for i in range(QUADS)]
             for m, tile in enumerate(swap_quads(tiles)):
                 out_ref[spot_ref[(n * groups + group) * QUADS + m]] = tile
-        return carry
-
-    lax.fori_loop(0, chunks, chunk, 0)
 
 
 def weights_call(order, stations, weight):
     count = order.shape[0]
     depth, observers = weight.shape
-    width = 512
     return pl.pallas_call(
         weights_kernel,
         name="observers",
-        out_shape=jax.ShapeDtypeStruct((count, ROWS, LANES), jnp.float32),
+        out_shape=(
+            jax.ShapeDtypeStruct((count, ROWS, LANES), jnp.float32),
+            jax.ShapeDtypeStruct((1, count), jnp.float32),
+        ),
         in_specs=[IN_SMEM, IN_VMEM, ANY],
-        out_specs=IN_VMEM,
+        out_specs=(IN_VMEM, IN_VMEM),
         scratch_shapes=[
             pltpu.VMEM((NT, depth), jnp.bfloat16),
-            pltpu.VMEM((observers // width, depth, width), jnp.bfloat16),
+            pltpu.VMEM((observers // WIDTH, depth, WIDTH), jnp.bfloat16),
             pltpu.SMEM((count,), jnp.int32),
-            pltpu.SemaphoreType.DMA((observers // width,)),
+            pltpu.SemaphoreType.DMA((observers // WIDTH,)),
         ],
         compiler_params=limits(14),
         cost_estimate=cost(2 * NT * depth * observers, 2 * depth * observers),
@@ -707,13 +703,6 @@
     return lax.ppermute(last, axis, up), lax.ppermute(first, axis, down)
 
 
-def neighbours(packed):
-    az_first, az_last, rad_first, rad_last = packed
-    rad = exchange(rad_first, rad_last, "radius", False)
-    az = exchange(az_first, az_last, "azimuth", True)
-    return az, rad
-
-
 def per_device(
     flow_state,
     base_state,
@@ -727,23 +716,28 @@
     retarded_time,
     observer_block,
 ):
-    az0, rad0 = neighbours(pack_call(flow_state, FIRST_AZ, FIRST_RAD))
-    slots = (panel_owner, panel_count.T)
-    history, local, coef = panels_call(
-        *slots, panel_line, mean_flow, flow_state, base_state, panel_history[0, 0]
+    az_first, az_last, *ends = pack_call(flow_state, FIRST_RAD, True)
+    az = exchange(az_first, az_last, "azimuth", True)
+    rad0 = exchange(*ends, "radius", False)
+    history, local, coef, slots = panels_call(
+        panel_owner,
+        panel_count.T,
+        panel_line,
+        mean_flow,
+        flow_state,
+        base_state,
+        panel_history[0, 0],
     )
-    outgoing = fresh_call(*slots, panel_line, panel_start, coef, local, az0, rad0, history)
+    outgoing = fresh_call(slots, panel_line, panel_start, coef, local, az, rad0, history)
     stations = lax.all_to_all(outgoing, "azimuth", split_axis=0, concat_axis=0, tiled=True)
     later, _ = lax.optimization_barrier((flow_state, outgoing))
-    packed = pack_call(later, LATER_AZ, LATER_RAD)
-    az1, rad1 = neighbours(packed)
-    sends = weights_call(observer_block, stations, source_weight[0])
+    packed = pack_call(later, LATER_RAD, False)
+    rad1 = exchange(*packed, "radius", False)
+    sends, mask = weights_call(observer_block, stations, source_weight[0])
     parts = lax.all_to_all(sends, BOTH, split_axis=0, concat_axis=0, tiled=True)
-    next_state = fields_call(flow_state, az0, az1, base_state, rad0, rad1, coef)
-
-    chosen = lax.dynamic_index_in_dim(observer_block, lax.axis_index(BOTH), 0, keepdims=False)
-    blocks = lax.broadcasted_iota(jnp.int32, retarded_time.shape, 0)
-    matrix = jnp.sum(jnp.where(blocks == chosen, retarded_time, 0.0), axis=0)
+    next_state = fields_call(flow_state, az, base_state, rad0, rad1, coef)
+
+    matrix = jnp.sum(retarded_time * mask[0][:, None, None], axis=0)
     pressure = retard_call(parts, matrix)
     return next_state, pressure.reshape(1, ROWS * LANES)
 

time: 90.7 us -> 79.4 us (0.88)
  the two profiles are of different devices: /device:TPU:0 before, /device:TPU:5 now
where the time goes in v3:
time: 79.4 us; the launch traced here: 79 us
  Pallas kernels  27 us (34%)
  starting transfers between devices  20 us (25%)
  blocking collectives  17.8 us (22%)
  waiting for transfers between devices  12.7 us (16%)
  between operations  0.87 us (1%)
    all_to_all x1, blocking collectives, per_device(): lax.all_to_all(outgoing, 'azimuth', split_axis=0, concat_axis=0, tiled=True)  17.8 us
    ppermute x6, starting transfers between devices, exchange(): return (lax.ppermute(last, axis, up), lax.ppermute(first, axis, down))  14.6 us
    ppermute x6, waiting for transfers between devices, exchange(): return (lax.ppermute(last, axis, up), lax.ppermute(first, axis, down))  12.7 us
    pallas_call x1, Pallas kernels, fields_call(): pl.pallas_call(fields_kernel, name='fields', out_shape=jax.ShapeDtypeStru...  11.3 us
    pallas_call x1, Pallas kernels, weights_call(): pl.pallas_call(weights_kernel, name='observers', out_shape=(jax.ShapeDtyp...  6.48 us
    all_to_all x1, starting transfers between devices, per_device(): parts = lax.all_to_all(sends, BOTH, split_axis=0, concat_axis=0, tiled=True)  5.41 us
    pallas_call x1, Pallas kernels, panels_call(): pl.pallas_call(panels_kernel, name='panels', out_shape=(jax.ShapeDtypeStr...  3.8 us
    pallas_call x2, Pallas kernels, pack_call(): pl.pallas_call(functools.partial(pack_kernel, rad=rad, with_az=with_az),...  3.3 us
  transfers between devices with their start and end apart: 7, of which 2 were waited for; matrix products, arithmetic and copies ran while one was open for 1% of the time, Pallas kernels for 21%

profile of v3, /device:TPU:5, one launch (start us, length us, event | category | flops | bytes accessed | tf_op | source)
XLA Modules:
  0.0 79.0 jit_solution(13612041132469809824)
XLA Ops:
  0.7 1.6 %shard_map.122 = (f32[5,2,32,384]{3,2,1,0:T(8,128)S(1)}, f32[5,2,32,384]{3,2,1,0:T(8,128)S(1)}, f32[16,4,384]{2,1,0:T(4,128)S(1)}, f32[16,4,384]{2,1,0:T(4,128)S(1)}) custom-call(f32[5,16,32,384]{3,2,1,0:T(8,128)} %flow_ref.6), custom_call_target="tpu_custom_call" | custom-call | bytes 20971520 | tf_op jit(solution)/shard_map/pallas_call | solution.py:507
  2.3 2.3 %collective-permute-start = (f32[5,2,32,384]{3,2,1,0:T(8,128)S(1)}, f32[5,2,32,384]{3,2,1,0:T(8,128)S(1)}, u32[]{:S(2)}, u32[]{:S(2)}) collective-permute-start(f32[5,2,32,384]{3,2,1,0:T(8,128)S(1)} %get-tuple-element.15), channel_id=1, source_target_pairs={{0,8},{8,16},{16,24},{24,32},{32,40},{40,48},{48,56},{56,64},{64,7... | collective-permute-start | bytes 1474568 | tf_op jit(solution)/shard_map/ppermute | solution.py:703
  4.6 0.0 collective-permute-start.1
  4.6 3.2 %collective-permute-start.2 = (f32[16,4,384]{2,1,0:T(4,128)S(1)}, f32[16,4,384]{2,1,0:T(4,128)S(1)}, u32[]{:S(2)}, u32[]{:S(2)}) collective-permute-start(f32[16,4,384]{2,1,0:T(4,128)S(1)} %get-tuple-element.17), channel_id=1, source_target_pairs={{0,1},{1,2},{2,3},{3,4},{4,5},{5,6},{6,7},{8,9},{9,10},{10,11},{11... | collective-permute-start | bytes 294920 | tf_op jit(solution)/shard_map/ppermute | solution.py:703
  7.8 3.0 %collective-permute-start.3 = (f32[16,4,384]{2,1,0:T(4,128)S(1)}, f32[16,4,384]{2,1,0:T(4,128)S(1)}, u32[]{:S(2)}, u32[]{:S(2)}) collective-permute-start(f32[16,4,384]{2,1,0:T(4,128)S(1)} %get-tuple-element.18), channel_id=1, source_target_pairs={{1,0},{2,1},{3,2},{4,3},{5,4},{6,5},{7,6},{9,8},{10,9},{11,10},{12... | collective-permute-start | bytes 294920 | tf_op jit(solution)/shard_map/ppermute | solution.py:703
  10.8 0.0 copy-start.4
  10.8 0.0 copy-start.5
  10.8 3.8 %panels.1 = (bf16[16,32,128]{2,1,0:T(8,128)(2,1)S(1)}, f32[16,8,128]{2,1,0:T(8,128)S(1)}, f32[11,32,128]{2,1,0:T(8,128)S(1)}, s32[128]{0:T(128)S(1)}) custom-call(s32[16,8,16]{2,1,0:T(8,128)} %owner_ref.1, s32[8,16]{1,0:T(8,128)S(1)} %bitcast.6, s32[1,1,16]{2,1,0:T(1,128)S(1)} %copy-done.2, f32[2,32]{1,0:T(2,128)S(1)} %copy-done.3, ...), custom_call_target="tpu_custom_call" | custom-call | bytes 3932160 | tf_op jit(solution)/shard_map/panels/pallas_call | solution.py:524
  14.6 0.0 collective-permute-done.2.lo_ref.lo0_ref
  14.7 0.0 collective-permute-done.1.after_ref
  14.7 1.0 %fresh.1 = bf16[16,32,128]{2,1,0:T(8,128)(2,1)S(1)} custom-call(s32[128]{0:T(128)S(1)} %get-tuple-element.19.slots_ref, s32[1,1,16]{2,1,0:T(1,128)S(1)} %copy-done.2, s32[1,1,16]{2,1,0:T(1,128)S(1)} %copy-done.4, f32[11,32,128]{2,1,0:T(8,128)S(1)} %get-tuple-element.20.coef_ref, f32[16,8,128]{2,1,0:T(8,128)S(1)} %get-tuple-element.21.rows_ref, ...), custom_call_target="tpu_custom_call" | custom-call | bytes 786432 | tf_op jit(solution)/shard_map/fresh/pallas_call | solution.py:551
  15.7 17.8 %all_to_all.10.stations_ref = bf16[16,32,128]{2,1,0:T(8,128)(2,1)S(1)} all-to-all(bf16[16,32,128]{2,1,0:T(8,128)(2,1)S(1)} %fresh.1), channel_id=1, replica_groups=mesh['azimuth'=16,'radius'=8] {'azimuth'}, dimensions={0} | all-to-all | bytes 262144 | tf_op jit(solution)/shard_map/all_to_all | solution.py:732
  33.5 6.5 %observers.1 = (f32[128,16,128]{2,1,0:T(8,128)}, f32[1,128]{1,0:T(1,128)S(1)}) custom-call(s32[128]{0:T(128)S(1)} %copy-done.5, bf16[16,32,128]{2,1,0:T(8,128)(2,1)S(1)} %all_to_all.10.stations_ref, bf16[1024,4096]{1,0:T(8,128)(2,1)} %bitcast.8), custom_call_target="tpu_custom_call" | custom-call | flops 536870912 | bytes 8388608 | tf_op jit(solution)/shard_map/observers/pallas_call | solution.py:640
  40.0 5.4 %all-to-all-start.1 = ((f32[128,16,128]{2,1,0:T(8,128)}), f32[128,16,128]{2,1,0:T(8,128)S(1)}, u32[]{:S(2)}, u32[]{:S(2)}) async-start(f32[128,16,128]{2,1,0:T(8,128)} %get-tuple-element.26), calls=%async_computation.1 | async-start | bytes 2097152 | tf_op jit(solution)/shard_map/all_to_all | solution.py:737
  45.4 0.0 copy-start.6
  45.4 1.7 %shard_map.123 = (f32[16,6,384]{2,1,0:T(8,128)S(1)}, f32[16,6,384]{2,1,0:T(8,128)S(1)}) custom-call(f32[5,16,32,384]{3,2,1,0:T(8,128)} %flow_ref.6), custom_call_target="tpu_custom_call" | custom-call | bytes 20971520 | tf_op jit(solution)/shard_map/pallas_call | solution.py:507
  47.1 3.1 %collective-permute-start.4 = (f32[16,6,384]{2,1,0:T(8,128)S(1)}, f32[16,6,384]{2,1,0:T(8,128)S(1)}, u32[]{:S(2)}, u32[]{:S(2)}) collective-permute-start(f32[16,6,384]{2,1,0:T(8,128)S(1)} %get-tuple-element.24), channel_id=1, source_target_pairs={{0,1},{1,2},{2,3},{3,4},{4,5},{5,6},{6,7},{8,9},{9,10},{10,11},{11... | collective-permute-start | bytes 442376 | tf_op jit(solution)/shard_map/ppermute | solution.py:703
  50.2 3.1 %collective-permute-start.5 = (f32[16,6,384]{2,1,0:T(8,128)S(1)}, f32[16,6,384]{2,1,0:T(8,128)S(1)}, u32[]{:S(2)}, u32[]{:S(2)}) collective-permute-start(f32[16,6,384]{2,1,0:T(8,128)S(1)} %get-tuple-element.25), channel_id=1, source_target_pairs={{1,0},{2,1},{3,2},{4,3},{5,4},{6,5},{7,6},{9,8},{10,9},{11,10},{12... | collective-permute-start | bytes 442376 | tf_op jit(solution)/shard_map/ppermute | solution.py:703
  53.3 0.6 multiply_reduce_fusion.matrix_ref
  53.9 10.8 %collective-permute-done.4.lo1_ref = f32[16,6,384]{2,1,0:T(8,128)S(1)} collective-permute-done((f32[16,6,384]{2,1,0:T(8,128)S(1)}, f32[16,6,384]{2,1,0:T(8,128)S(1)}, u32[]{:S(2)}, u32[]{:S(2)}) %collective-permute-start.4) | collective-permute-done | bytes 147488 | tf_op jit(solution)/shard_map/ppermute | solution.py:703
  64.7 1.9 %collective-permute-done.5.hi1_ref = f32[16,6,384]{2,1,0:T(8,128)S(1)} collective-permute-done((f32[16,6,384]{2,1,0:T(8,128)S(1)}, f32[16,6,384]{2,1,0:T(8,128)S(1)}, u32[]{:S(2)}, u32[]{:S(2)}) %collective-permute-start.5) | collective-permute-done | bytes 147488 | tf_op jit(solution)/shard_map/ppermute | solution.py:703
  66.6 11.3 %fields.1 = f32[5,16,32,384]{3,2,1,0:T(8,128)} custom-call(f32[5,16,32,384]{3,2,1,0:T(8,128)} %flow_ref.6, f32[5,2,32,384]{3,2,1,0:T(8,128)S(1)} %collective-permute-done.before_ref, f32[5,2,32,384]{3,2,1,0:T(8,128)S(1)} %collective-permute-done.1.after_ref, f32[5,16,32,384]{3,2,1,0:T(8,128)} %base_ref.3, ...), custom_call_target="tpu_custom_call" | custom-call | flops 49152000 | bytes 11796480 | tf_op jit(solution)/shard_map/fields/pallas_call | solution.py:572
  77.9 0.0 all-to-all-done.1.parts_ref
  77.9 1.1 %retard.1 = f32[16,128]{1,0:T(8,128)} custom-call(f32[128,16,128]{2,1,0:T(8,128)S(1)} %all-to-all-done.1.parts_ref, f32[64,64]{1,0:T(8,128)S(1)} %multiply_reduce_fusion.matrix_ref), custom_call_target="tpu_custom_call" | custom-call | flops 524288 | bytes 1048576 | tf_op jit(solution)/shard_map/retard/pallas_call | solution.py:687
  (13 shorter events, 0.0 us)
Async XLA Ops:
  0.6 10.1 %copy-start.2 = (s32[1,1,16]{2,1,0:T(1,128)S(1)}, s32[1,1,16]{2,1,0:T(1,128)}, u32[]{:S(2)}) copy-start(s32[1,1,16]{2,1,0:T(1,128)} %line_ref.3) | copy-start | bytes 196
  0.6 10.1 %copy-start.1 = (s32[16,8]{0,1:T(8,128)S(1)}, s32[16,8]{0,1:T(8,128)}, u32[]{:S(2)}) copy-start(s32[16,8]{0,1:T(8,128)} %param.17) | copy-start | bytes 1540
  0.7 10.1 %copy-start = (bf16[1,1,16,2016]{3,2,1,0:T(8,128)(2,1)S(1)}, bf16[1,1,16,2016]{3,2,1,0:T(8,128)(2,1)}, u32[]{:S(2)}) copy-start(bf16[1,1,16,2016]{3,2,1,0:T(8,128)(2,1)} %param.14) | copy-start | bytes 193540
  0.7 10.1 %copy-start.3 = (f32[2,32]{1,0:T(2,128)S(1)}, f32[2,32]{1,0:T(2,128)}, u32[]{:S(2)}) copy-start(f32[2,32]{1,0:T(2,128)} %mean_ref.1) | copy-start | bytes 772
  2.3 12.3 %collective-permute-start = (f32[5,2,32,384]{3,2,1,0:T(8,128)S(1)}, f32[5,2,32,384]{3,2,1,0:T(8,128)S(1)}, u32[]{:S(2)}, u32[]{:S(2)}) collective-permute-start(f32[5,2,32,384]{3,2,1,0:T(8,128)S(1)} %get-tuple-element.15), channel_id=1, source_target_pairs={{0,8},{8,16},{16,24},{24,32},{32,40},{40,48},{48,56},{56,64},{64,7... | collective-permute-start | bytes 1474568 | tf_op jit(solution)/shard_map/ppermute | solution.py:703
  4.6 10.1 %collective-permute-start.1 = (f32[5,2,32,384]{3,2,1,0:T(8,128)S(1)}, f32[5,2,32,384]{3,2,1,0:T(8,128)S(1)}, u32[]{:S(2)}, u32[]{:S(2)}) collective-permute-start(f32[5,2,32,384]{3,2,1,0:T(8,128)S(1)} %get-tuple-element.16), channel_id=1, source_target_pairs={{8,0},{16,8},{24,16},{32,24},{40,32},{48,40},{56,48},{64,56},{72,6... | collective-permute-start | bytes 1474568 | tf_op jit(solution)/shard_map/ppermute | solution.py:703
  4.6 10.1 %collective-permute-start.2 = (f32[16,4,384]{2,1,0:T(4,128)S(1)}, f32[16,4,384]{2,1,0:T(4,128)S(1)}, u32[]{:S(2)}, u32[]{:S(2)}) collective-permute-start(f32[16,4,384]{2,1,0:T(4,128)S(1)} %get-tuple-element.17), channel_id=1, source_target_pairs={{0,1},{1,2},{2,3},{3,4},{4,5},{5,6},{6,7},{8,9},{9,10},{10,11},{11... | collective-permute-start | bytes 294920 | tf_op jit(solution)/shard_map/ppermute | solution.py:703
  7.8 6.9 %collective-permute-start.3 = (f32[16,4,384]{2,1,0:T(4,128)S(1)}, f32[16,4,384]{2,1,0:T(4,128)S(1)}, u32[]{:S(2)}, u32[]{:S(2)}) collective-permute-start(f32[16,4,384]{2,1,0:T(4,128)S(1)} %get-tuple-element.18), channel_id=1, source_target_pairs={{1,0},{2,1},{3,2},{4,3},{5,4},{6,5},{7,6},{9,8},{10,9},{11,10},{12... | collective-permute-start | bytes 294920 | tf_op jit(solution)/shard_map/ppermute | solution.py:703
  10.8 3.9 %copy-start.4 = (s32[1,1,16]{2,1,0:T(1,128)S(1)}, s32[1,1,16]{2,1,0:T(1,128)}, u32[]{:S(2)}) copy-start(s32[1,1,16]{2,1,0:T(1,128)} %start_ref.1) | copy-start | bytes 196
  10.8 22.7 %copy-start.5 = (s32[128]{0:T(128)S(1)}, s32[128]{0:T(128)}, u32[]{:S(2)}) copy-start(s32[128]{0:T(128)} %order_ref.1) | copy-start | bytes 1540
  40.0 38.0 %all-to-all-start.1 = ((f32[128,16,128]{2,1,0:T(8,128)}), f32[128,16,128]{2,1,0:T(8,128)S(1)}, u32[]{:S(2)}, u32[]{:S(2)}) async-start(f32[128,16,128]{2,1,0:T(8,128)} %get-tuple-element.26), calls=%async_computation.1 | async-start | bytes 2097152 | tf_op jit(solution)/shard_map/all_to_all | solution.py:737
  45.4 7.9 %copy-start.6 = (f32[128,64,64]{0,2,1:T(8,128)S(1)}, f32[128,64,64]{0,2,1:T(8,128)}, u32[]{:S(2)}) copy-start(f32[128,64,64]{0,2,1:T(8,128)} %param.20) | copy-start | bytes 6291460
  47.1 17.6 %collective-permute-start.4 = (f32[16,6,384]{2,1,0:T(8,128)S(1)}, f32[16,6,384]{2,1,0:T(8,128)S(1)}, u32[]{:S(2)}, u32[]{:S(2)}) collective-permute-start(f32[16,6,384]{2,1,0:T(8,128)S(1)} %get-tuple-element.24), channel_id=1, source_target_pairs={{0,1},{1,2},{2,3},{3,4},{4,5},{5,6},{6,7},{8,9},{9,10},{10,11},{11... | collective-permute-start | bytes 442376 | tf_op jit(solution)/shard_map/ppermute | solution.py:703
  50.2 16.4 %collective-permute-start.5 = (f32[16,6,384]{2,1,0:T(8,128)S(1)}, f32[16,6,384]{2,1,0:T(8,128)S(1)}, u32[]{:S(2)}, u32[]{:S(2)}) collective-permute-start(f32[16,6,384]{2,1,0:T(8,128)S(1)} %get-tuple-element.25), channel_id=1, source_target_pairs={{1,0},{2,1},{3,2},{4,3},{5,4},{6,5},{7,6},{9,8},{10,9},{11,10},{12... | collective-permute-start | bytes 442376 | tf_op jit(solution)/shard_map/ppermute | solution.py:703
